TPU v7x, 128 devices: a whole 4x4x4 slice. The times are simulated.
128 devices in a mesh: dof: 64 (over z, x, y_hi, core), snap: 2 (over y_lo).
Axes of the slice: x: 4, y: 4 (y_hi: 2, y_lo: 2; y = y_hi * 2 + y_lo), z: 4, core: 2. Of those that a mesh axis runs over, the one named last changes fastest.
Arguments:
- snapshots: float32 [262144, 1024], P('dof', 'snap'), may hold values from -19 to 19
Outputs:
- basis: float32 [262144, 1024], P('dof', 'snap')
- factor: float32 [1024, 1024], P(None, 'snap')
All inputs are finite; a program needn't handle non-finite values.
Results may differ from a plain program's by a relative error of at most 0.00024.
Values sent between devices are 32-bit elements; how exact they have to be, the bound alone decides.
A program may use at most 128 MiB of HBM per device.

v0:
```python
import functools

import jax
import jax.numpy as jnp
from jax import lax
from jax.experimental import pallas as pl
from jax.experimental.pallas import tpu as pltpu
from jax.sharding import PartitionSpec as P

MESH = pl.DeviceIdType.MESH
HI = lax.Precision.HIGHEST
T = 128

def dot_nt(a, b):
    return lax.dot_general(a, b, (((1,), (1,)), ((), ())), preferred_element_type=jnp.float32, precision=HI)

def dot_nn(a, b):
    return lax.dot_general(a, b, (((1,), (0,)), ((), ())), preferred_element_type=jnp.float32, precision=HI)

def eliminate(block):
    sub = lax.broadcasted_iota(jnp.int32, (8, T), 0)
    lane = lax.broadcasted_iota(jnp.int32, (8, T), 1)
    rows = [block[8 * i:8 * i + 8, :] for i in range(T // 8)]
    upper, lower, pivots = [], [], []
    for b in range(T // 8):
        first = 8 * b
        in_block = (lane >= first) & (lane < first + 8)
        head = rows[b]
        cols = [jnp.broadcast_to(head[:, first + k:first + k + 1], (8, T)) for k in range(8)]
        t = {}
        for k in range(8):
            for j in range(k + 1):
                t[j, k] = jnp.broadcast_to(cols[k][j:j + 1, :], (8, T))
        recip = []
        for j in range(8):
            r = 1.0 / t[j, j]
            recip.append(r)
            for k in range(j + 1, 8):
                s = t[j, k] * r
                for l in range(k, 8):
                    t[k, l] = t[k, l] - s * t[j, l]
        pivot = t[0, 0]
        for j in range(1, 8):
            pivot = jnp.where(sub == j, t[j, j], pivot)
        pivots.append(pivot)

        def multipliers(cs, below):
            cs = list(cs)
            out = []
            for j in range(8):
                m = cs[j] * recip[j]
                if not below:
                    m = jnp.where(sub > j, m, 0.0)
                out.append(m)
                for k in range(j + 1, 8):
                    cs[k] = cs[k] - m * t[j, k]
            return out

        v = jnp.where(in_block, jnp.where(lane == sub + first, 1.0, 0.0), head)
        m = multipliers(cols, False)
        own = head
        for j in range(8):
            v = v - m[j] * jnp.broadcast_to(v[j:j + 1, :], (8, T))
            own = own - m[j] * jnp.broadcast_to(own[j:j + 1, :], (8, T))
        vb = [jnp.broadcast_to(v[j:j + 1, :], (8, T)) for j in range(8)]
        upper.append(jnp.where(lane >= sub + first, own, 0.0))
        lower.append(jnp.where(lane <= sub + first, v, 0.0))
        for i in range(b + 1, T // 8):
            cs = [jnp.broadcast_to(rows[i][:, first + k:first + k + 1], (8, T)) for k in range(8)]
            m = multipliers(cs, True)
            w = jnp.where(in_block, 0.0, rows[i])
            for j in range(8):
                w = w - m[j] * vb[j]
            rows[i] = w
    cat = lambda x: jnp.concatenate(x, axis=0)
    return cat(lower), cat(upper), cat(pivots)

def factor_into(a_ref, l_ref, x_ref, n, lt_ref=None):
    steps = n // T
    def step(p, _):
        at = pl.ds(pl.multiple_of(p * T, T), T)
        low, up, piv = eliminate(a_ref[at, at])
        scale = lax.rsqrt(piv)
        xd = low * scale
        ld = up * scale
        x_ref[at, at] = xd
        l_ref[at, at] = ld.T
        for k in range(steps):
            @pl.when(p == k)
            def _():
                o = k * T
                e = o + T
                if k > 0:
                    part = dot_nn(l_ref[o:e, 0:o], x_ref[0:o, 0:o])
                    x_ref[o:e, 0:o] = -dot_nn(xd, part)
                if e < n:
                    x_ref[o:e, e:n] = jnp.zeros((T, n - e), jnp.float32)
                    l_ref[o:e, e:n] = jnp.zeros((T, n - e), jnp.float32)
                    l21 = dot_nt(a_ref[e:n, o:e], xd)
                    l_ref[e:n, o:e] = l21
                    a_ref[e:n, e:n] = a_ref[e:n, e:n] - dot_nt(l21, l21)
        return 0
    lax.fori_loop(0, steps, step, 0)


VMEM = pl.BlockSpec(memory_space=pltpu.VMEM)


def first_kernel(g_ref, l_ref, x_ref, a_ref):
    a_ref[...] = g_ref[0]
    factor_into(a_ref, l_ref, x_ref, g_ref.shape[1])


def factor_first(grams):
    n = grams.shape[1]
    square = jax.ShapeDtypeStruct((n, n), jnp.float32)
    return pl.pallas_call(
        first_kernel,
        out_shape=(square, square),
        in_specs=[VMEM],
        out_specs=(VMEM, VMEM),
        scratch_shapes=[pltpu.VMEM((n, n), jnp.float32)],
        compiler_params=pltpu.CompilerParams(vmem_limit_bytes=40 << 20),
        cost_estimate=pl.CostEstimate(flops=24 << 30, bytes_accessed=80 << 20, transcendentals=0),
    )(grams)


def second_kernel(g_ref, c_ref, xa_ref, lba_ref, xba_ref, l_ref, x_ref, a_ref):
    n = xa_ref.shape[0]
    lba = dot_nt(c_ref[0], xa_ref[...])
    lba_ref[...] = lba
    a_ref[...] = g_ref[1] - dot_nt(lba, lba)
    factor_into(a_ref, l_ref, x_ref, n)
    xba_ref[...] = -dot_nn(x_ref[...], dot_nn(lba_ref[...], xa_ref[...]))


def factor_second(grams, cross, xa):
    n = xa.shape[0]
    square = jax.ShapeDtypeStruct((n, n), jnp.float32)
    return pl.pallas_call(
        second_kernel,
        out_shape=(square,) * 4,
        in_specs=[VMEM] * 3,
        out_specs=(VMEM,) * 4,
        scratch_shapes=[pltpu.VMEM((n, n), jnp.float32)],
        compiler_params=pltpu.CompilerParams(vmem_limit_bytes=40 << 20),
        cost_estimate=pl.CostEstimate(flops=24 << 30, bytes_accessed=80 << 20, transcendentals=0),
    )(grams, cross, xa)


def place():
    dof, snap = lax.axis_index("dof"), lax.axis_index("snap")
    core, y_hi = lax.rem(dof, 2), lax.rem(dof // 2, 2)
    return dof // 16, lax.rem(dof // 4, 4), y_hi * 2 + snap, core


def device(z, x, y, core):
    return (z * 16 + x * 4 + (y // 2) * 2 + core, lax.rem(y, 2))


def neighbours(with_y):
    z, x, y, core = place()
    over_core = [device(z, x, y, 1 - core)]
    over_x = [device(z, lax.rem(x + k, 4), y, core) for k in (1, 2, 3)]
    over_z = [device(lax.rem(z + k, 4), x, y, core) for k in (1, 2, 3)]
    down = device(z, x, lax.rem(y + 3, 4), core)
    greet = over_core + over_x + over_z
    if with_y:
        greet = greet + [down, device(z, x, lax.rem(y + 1, 4), core)]
    barrier = pltpu.get_barrier_semaphore()
    for partner in greet:
        pl.semaphore_signal(barrier, inc=1, device_id=partner, device_id_type=MESH)
    pl.semaphore_wait(barrier, len(greet))
    return over_core, over_x, over_z, down


class Sender:
    def __init__(self, send_sem, recv_sem):
        self.sems, self.used = (send_sem, recv_sem), 0

    def start(self, src, dst, to):
        send_sem, recv_sem = (s.at[self.used] for s in self.sems)
        self.used += 1
        copy = pltpu.make_async_remote_copy(
            src_ref=src, dst_ref=dst, send_sem=send_sem, recv_sem=recv_sem, device_id=to, device_id_type=MESH)
        copy.start()
        return copy

    def run(self, triples):
        for copy in [self.start(*t) for t in triples]:
            copy.wait()


def rows(start, size):
    return pl.ds(pl.multiple_of(start, size), size)


def scatter_sum(send, where, p_ref, half, quarter, piece, rc, rx, rz, ry):
    over_core, over_x, over_z, down = where
    z, x, y, core = place()
    n = p_ref.shape[0]
    h, q, s = n // 2, n // 8, n // 32
    send.run([(p_ref.at[rows((1 - core) * h, h)], rc, over_core[0])])
    half[...] = p_ref[rows(core * h, h), :] + rc[...]
    send.run([(half.at[rows(lax.rem(x + k, 4) * q, q)], rx.at[k - 1], over_x[k - 1]) for k in (1, 2, 3)])
    quarter[...] = (half[rows(x * q, q), :] + rx[1]) + (rx[0] + rx[2])
    send.run([(quarter.at[rows(lax.rem(z + k, 4) * s, s)], rz.at[k - 1], over_z[k - 1]) for k in (1, 2, 3)])
    ry[y] = (quarter[rows(z * s, s), :] + rz[1]) + (rz[0] + rz[2])
    for k in (0, 1, 2):
        slot = ry.at[lax.rem(y + k, 4)]
        send.run([(slot, slot, down)])


def gather_rows(send, where, out_ref):
    over_core, over_x, over_z, down = where
    z, x, y, core = place()
    n = out_ref.shape[1]
    h, q, s = n // 2, n // 8, n // 32
    base = core * h + x * q
    part = out_ref.at[:, rows(base + z * s, s)]
    send.run([(part, part, over_z[k - 1]) for k in (1, 2, 3)])
    part = out_ref.at[:, rows(base, q)]
    send.run([(part, part, over_x[k - 1]) for k in (1, 2, 3)])
    part = out_ref.at[:, rows(core * h, h)]
    send.run([(part, part, over_core[0])])


def own_rows(n):
    z, x, y, core = place()
    s = n // 32
    return rows(core * (n // 2) + x * (n // 8) + z * s, s)


def scatter_kernel(p_ref, out_ref, half, quarter, piece, rc, rx, rz, ry, send_sem, recv_sem):
    where = neighbours(True)
    scatter_sum(Sender(send_sem, recv_sem), where, p_ref, half, quarter, piece, rc, rx, rz, ry)
    out_ref[0] = ry[0] + ry[2]
    out_ref[1] = ry[1] + ry[3]


def gather_kernel(p_ref, out_ref, send_sem, recv_sem):
    where = neighbours(False)
    out_ref[:, own_rows(out_ref.shape[1]), :] = p_ref[...]
    gather_rows(Sender(send_sem, recv_sem), where, out_ref)


def reduce_kernel(p_ref, out_ref, half, quarter, piece, rc, rx, rz, ry, send_sem, recv_sem):
    where = neighbours(True)
    send = Sender(send_sem, recv_sem)
    scatter_sum(send, where, p_ref, half, quarter, piece, rc, rx, rz, ry)
    out_ref[0, own_rows(out_ref.shape[1]), :] = (ry[0] + ry[2]) + (ry[1] + ry[3])
    gather_rows(send, where, out_ref)


def scratch(n, copies):
    f32 = jnp.float32
    return [
        pltpu.VMEM((n // 2, n), f32),
        pltpu.VMEM((n // 8, n), f32),
        pltpu.VMEM((n // 32, n), f32),
        pltpu.VMEM((n // 2, n), f32),
        pltpu.VMEM((3, n // 8, n), f32),
        pltpu.VMEM((3, n // 32, n), f32),
        pltpu.VMEM((4, n // 32, n), f32),
        pltpu.SemaphoreType.DMA((copies,)),
        pltpu.SemaphoreType.DMA((copies,)),
    ]


def talk(kernel, out_shape, scratch_shapes, collective_id, operand):
    return pl.pallas_call(
        kernel,
        out_shape=jax.ShapeDtypeStruct(out_shape, jnp.float32),
        in_specs=[VMEM],
        out_specs=VMEM,
        scratch_shapes=scratch_shapes,
        compiler_params=pltpu.CompilerParams(
            collective_id=collective_id, has_side_effects=True, vmem_limit_bytes=40 << 20),
        cost_estimate=pl.CostEstimate(flops=32 << 30, bytes_accessed=100 << 20, transcendentals=0),
    )(operand)


def split(x):
    high = x.astype(jnp.bfloat16)
    return high, (x - high.astype(jnp.float32)).astype(jnp.bfloat16)


def dot3(a, b, over):
    dims = ((over[:1], over[1:]), ((), ()))
    dot = lambda l, r: lax.dot_general(l, r, dims, preferred_element_type=jnp.float32)
    return dot(a[0], b[0]) + (dot(a[0], b[1]) + dot(a[1], b[0]))


CHUNK = 256


def cross_kernel(early, who_ref, own_ref, a_ref, b1_ref, b2_ref, out_ref):
    i = pl.program_id(0)
    second = who_ref[0] == 1
    got = jnp.where(second, a_ref[...], jnp.where(i < early, b1_ref[...], b2_ref[...]))
    own = own_ref[...]
    left = split(jnp.where(second, own, got))
    right = split(jnp.where(second, got, own))

    @pl.when(i == 0)
    def _():
        out_ref[...] = jnp.zeros_like(out_ref)

    out_ref[...] += dot3(left, right, (0, 0))


def cross_gram(snap, own, a, b1, b2):
    steps, n = a.shape[0] // CHUNK, own.shape[1]
    early, late = b1.shape[0] // CHUNK, b2.shape[0] // CHUNK
    block = lambda index: pl.BlockSpec((CHUNK, n), index)
    return pl.pallas_call(
        functools.partial(cross_kernel, early),
        out_shape=jax.ShapeDtypeStruct((n, n), jnp.float32),
        grid_spec=pltpu.PrefetchScalarGridSpec(
            num_scalar_prefetch=1,
            grid=(steps,),
            in_specs=[
                block(lambda i, who: ((1 - who[0]) * steps + i, 0)),
                block(lambda i, who: (who[0] * i, 0)),
                block(lambda i, who: ((1 - who[0]) * jnp.minimum(i, early - 1), 0)),
                block(lambda i, who: ((1 - who[0]) * jnp.clip(i - early, 0, late - 1), 0)),
            ],
            out_specs=pl.BlockSpec((n, n), lambda i, who: (0, 0)),
        ),
        compiler_params=pltpu.CompilerParams(vmem_limit_bytes=40 << 20),
        cost_estimate=pl.CostEstimate(flops=3 << 30, bytes_accessed=12 << 20, transcendentals=0),
    )(snap, own, a, b1, b2)


TALL = 512


def basis_kernel(scale, who_ref, own_ref, a_ref, xa_ref, xb_ref, xba_ref, *others):
    out_ref, high, low, high2, low2 = others[-5:]
    second = who_ref[0] == 1

    @pl.when(pl.program_id(0) == 0)
    def _():
        high[...], low[...] = split(jnp.where(second, xb_ref[...], xa_ref[...]) * scale)
        high2[...], low2[...] = split(xba_ref[...] * scale)

    out_ref[...] = dot3(split(own_ref[...]), (high[...], low[...]), (1, 1))

    @pl.when(second)
    def _():
        out_ref[...] += dot3(split(a_ref[...]), (high2[...], low2[...]), (1, 1))


def basis_rows(scale, first_row, snap, own, a, xa, xb, xba, so_far):
    count, n = own.shape
    steps, offset = a.shape[0] // TALL, first_row // TALL
    whole = pl.BlockSpec((n, n), lambda i, who: (0, 0))
    placed = pl.BlockSpec((TALL, n), lambda i, who: (i + offset, 0))
    extra = [] if so_far is None else [so_far]
    return pl.pallas_call(
        functools.partial(basis_kernel, scale),
        out_shape=jax.ShapeDtypeStruct((count, n), jnp.float32),
        grid_spec=pltpu.PrefetchScalarGridSpec(
            num_scalar_prefetch=1,
            grid=(steps,),
            in_specs=[placed, pl.BlockSpec((TALL, n), lambda i, who: (who[0] * i, 0)), whole, whole, whole]
            + [pl.BlockSpec(memory_space=pl.ANY)] * len(extra),
            out_specs=placed,
            scratch_shapes=[pltpu.VMEM((n, n), jnp.bfloat16)] * 4,
        ),
        input_output_aliases={6: 0} if extra else {},
        compiler_params=pltpu.CompilerParams(vmem_limit_bytes=40 << 20),
        cost_estimate=pl.CostEstimate(flops=6 << 30, bytes_accessed=12 << 20, transcendentals=0),
    )(snap, own, a, xa, xb, xba, *extra)


def on_device(snapshots):
    count, n = snapshots.shape
    snap = lax.axis_index("snap")
    first = snap == 0
    who = snap.astype(jnp.int32).reshape(1)
    rows_in_all = count * lax.axis_size("dof")
    root_rows = float(rows_in_all) ** 0.5
    mid = count // 2
    early = mid + 3 * CHUNK

    tie = lambda *values: lax.optimization_barrier(values)
    a1 = lax.ppermute(snapshots[:mid], "snap", [(0, 1)])
    b1 = lax.ppermute(snapshots[mid:early], "snap", [(1, 0)])
    own_gram = lax.dot_general(
        snapshots, snapshots, (((0,), (0,)), ((), ())), preferred_element_type=jnp.float32, precision=lax.Precision.HIGH)
    pieces = talk(scatter_kernel, (2, n // 32, n), scratch(n, 10), 0, own_gram)
    b1, pieces = tie(b1, pieces)
    late, pieces = tie(snapshots, pieces)
    b2 = lax.ppermute(late[early:], "snap", [(1, 0)])
    a2 = lax.ppermute(late[mid:], "snap", [(0, 1)])
    grams = talk(gather_kernel, (2, n, n), scratch(n, 7)[-2:], 1, pieces)
    la, xa = factor_first(grams)

    a1, b1, b2, la = tie(a1, b1, b2, la)
    cross = cross_gram(who, snapshots, a1, b1, b2)
    cross = talk(reduce_kernel, (1, n, n), scratch(n, 17), 2, cross)
    lba, xba, lb, xb = factor_second(grams, cross, xa)

    basis = basis_rows(root_rows, 0, who, snapshots, a1, xa, xb, xba, None)
    a2, basis = tie(a2, basis)
    basis = basis_rows(root_rows, mid, who, snapshots, a2, xa, xb, xba, basis)
    top = jnp.where(first, la, lba).T
    bottom = jnp.where(first, 0.0, lb).T
    factor = jnp.concatenate([top, bottom]) / root_rows
    return (basis, factor)


def solution(mesh):
    in_specs = (P("dof", "snap"),)
    out_specs = (P("dof", "snap"), P(None, "snap"))
    return jax.shard_map(
        on_device, mesh=mesh, in_specs=in_specs, out_specs=out_specs, check_vma=False
    )
```

profile of v0, /device:TPU:9, one launch (start us, length us, event | category | flops | bytes accessed | tf_op | source)
XLA Modules:
  0.0 215.3 jit_solution(18060651341468171927)
XLA Ops:
  0.6 2.7 %slice.12 = f32[768,512]{1,0:T(8,128)} slice(f32[4096,512]{1,0:T(8,128)} %own_ref.5), slice={[2048:2816], [0:512]} | slice | bytes 3145728 | tf_op jit(solution)/shard_map/slice | solution.py:389
  3.3 1.7 collective-permute-start
  5.0 5.3 %slice.14 = f32[2048,512]{1,0:T(8,128)} slice(f32[4096,512]{1,0:T(8,128)} %own_ref.5), slice={[0:2048], [0:512]} | slice | bytes 8388608 | tf_op jit(solution)/shard_map/slice | solution.py:388
  10.3 1.3 collective-permute-start.2
  11.6 6.7 %fusion.p_ref = f32[512,512]{1,0:T(8,128)S(1)} fusion(f32[4096,512]{1,0:T(8,128)S(1)} %copy-done), kind=kOutput, calls=%fused_computation.3 | convolution fusion | flops 6442450944 | bytes 9437184 | tf_op jit(solution)/shard_map/dot_general | solution.py:390
  18.3 30.1 %shard_map.30.p_ref = f32[2,16,512]{2,1,0:T(8,128)S(1)} custom-call(f32[512,512]{1,0:T(8,128)S(1)} %fusion.p_ref), custom_call_target="tpu_custom_call" | custom-call | flops 34359738368 | bytes 104857600 | tf_op jit(solution)/shard_map/pallas_call | solution.py:271
  48.5 0.0 collective-permute-done.b1_ref
  48.5 0.0 slice-start
  48.5 2.1 slice.15
  50.6 0.0 slice-start.1
  50.7 3.0 %collective-permute-start.3 = (f32[1280,512]{1,0:T(8,128)S(1)}, f32[1280,512]{1,0:T(8,128)S(1)}, u32[]{:S(2)}, u32[]{:S(2)}) collective-permute-start(f32[1280,512]{1,0:T(8,128)S(1)} %slice.15), channel_id=1, source_target_pairs={{1,0},{3,2},{5,4},{7,6},{9,8},{11,10},{13,12},{15,14},{17,16},{19,... | collective-permute-start | bytes 7864328 | tf_op jit(solution)/shard_map/ppermute | solution.py:395
  53.7 26.2 %shard_map.31.g_ref = f32[2,512,512]{2,1,0:T(8,128)S(1)} custom-call(f32[2,16,512]{2,1,0:T(8,128)S(1)} %shard_map.30.p_ref), custom_call_target="tpu_custom_call" | custom-call | flops 34359738368 | bytes 104857600 | tf_op jit(solution)/shard_map/pallas_call | solution.py:271
  79.9 2.4 %slice.13 = f32[2048,512]{1,0:T(8,128)} slice(f32[4096,512]{1,0:T(8,128)S(1)} %bitcast.8), slice={[2048:4096], [0:512]} | slice | bytes 8388608 | tf_op jit(solution)/shard_map/slice | solution.py:396
  82.3 1.5 collective-permute-start.1
  83.8 20.3 %shard_map.32 = (f32[512,512]{1,0:T(8,128)S(1)}, f32[512,512]{1,0:T(8,128)S(1)}) custom-call(f32[2,512,512]{2,1,0:T(8,128)S(1)} %shard_map.31.g_ref), custom_call_target="tpu_custom_call" | custom-call | flops 25769803776 | bytes 83886080 | tf_op jit(solution)/shard_map/pallas_call | solution.py:117
  104.1 1.8 collective-permute-done.3.b2_ref
  105.9 9.6 %shard_map.33.p_ref = f32[512,512]{1,0:T(8,128)S(1)} custom-call(s32[1]{0:T(128)} %bitcast.who_ref, f32[4096,512]{1,0:T(8,128)} %own_ref.5, f32[2048,512]{1,0:T(8,128)} %collective-permute-done.2.a_ref, f32[768,512]{1,0:T(8,128)S(1)} %collective-permute-done.b1_ref, f32[1280,512]{1,0:T(8,128)S(1)} %collective-permute-done.3.b2_ref), custom_call_target="tpu_custom_call" | custom-call | flops 3221225472 | bytes 12582912 | tf_op jit(solution)/shard_map/pallas_call | solution.py:316
  115.5 44.8 %shard_map.34.c_ref = f32[1,512,512]{2,1,0:T(8,128)S(1)} custom-call(f32[512,512]{1,0:T(8,128)S(1)} %shard_map.33.p_ref), custom_call_target="tpu_custom_call" | custom-call | flops 34359738368 | bytes 104857600 | tf_op jit(solution)/shard_map/pallas_call | solution.py:271
  160.3 27.7 %shard_map.35 = (f32[512,512]{1,0:T(8,128)S(1)}, f32[512,512]{1,0:T(8,128)S(1)}, f32[512,512]{1,0:T(8,128)S(1)}, f32[512,512]{1,0:T(8,128)S(1)}) custom-call(f32[2,512,512]{2,1,0:T(8,128)S(1)} %shard_map.31.g_ref, f32[1,512,512]{2,1,0:T(8,128)S(1)} %shard_map.34.c_ref, f32[512,512]{1,0:T(8,128)S(1)} %get-tuple-element.24.xa_ref), custom_call_target="tpu_custom_call" | custom-call | flops 25769803776 | bytes 83886080 | tf_op jit(solution)/shard_map/pallas_call | solution.py:140
  188.0 0.3 select_bitcast_fusion
  188.4 1.5 maximum_multiply_fusion
  189.9 2.9 %copy.4 = f32[1024,512]{1,0:T(8,128)} copy(f32[1024,512]{0,1:T(8,128)} %maximum_multiply_fusion) | data formatting | bytes 4194304
  192.8 11.3 %shard_map.36.others_0_ = f32[4096,512]{1,0:T(8,128)} custom-call(s32[1]{0:T(128)} %bitcast.who_ref, f32[4096,512]{1,0:T(8,128)} %own_ref.5, f32[2048,512]{1,0:T(8,128)} %collective-permute-done.2.a_ref, f32[512,512]{1,0:T(8,128)S(1)} %get-tuple-element.24.xa_ref, f32[512,512]{1,0:T(8,128)S(1)} %get-tuple-element.27.xb_ref, ...), custom_call_target="tpu_custom_call" | custom-call | flops 6442450944 | bytes 12582912 | tf_op jit(solution)/shard_map/pallas_call | solution.py:360
  204.1 11.3 %shard_map.37 = f32[4096,512]{1,0:T(8,128)} custom-call(s32[1]{0:T(128)} %bitcast.who_ref, f32[4096,512]{1,0:T(8,128)} %own_ref.5, f32[2048,512]{1,0:T(8,128)} %collective-permute-done.1.a_ref, f32[512,512]{1,0:T(8,128)S(1)} %get-tuple-element.24.xa_ref, f32[512,512]{1,0:T(8,128)S(1)} %get-tuple-element.27.xb_ref, ...), custom_call_target="tpu_custom_call", output_to_operand_aliasing={{}: (6, {})} | custom-call | flops 6442450944 | bytes 12582912 | tf_op jit(solution)/shard_map/pallas_call | solution.py:360
  (7 shorter events, 0.0 us)
Async XLA Ops:
  3.3 8.3 %copy-start = (f32[4096,512]{1,0:T(8,128)S(1)}, f32[4096,512]{1,0:T(8,128)}, u32[]{:S(2)}) copy-start(f32[4096,512]{1,0:T(8,128)} %own_ref.5) | copy-start | bytes 25165828
  3.3 45.2 %collective-permute-start = (f32[768,512]{1,0:T(8,128)}, f32[768,512]{1,0:T(8,128)S(1)}, u32[]{:S(2)}, u32[]{:S(2)}) collective-permute-start(f32[768,512]{1,0:T(8,128)} %slice.12), channel_id=1, source_target_pairs={{1,0},{3,2},{5,4},{7,6},{9,8},{11,10},{13,12},{15,14},{17,16},{19,... | collective-permute-start | bytes 4718600 | tf_op jit(solution)/shard_map/ppermute | solution.py:389
  10.3 95.6 %collective-permute-start.2 = (f32[2048,512]{1,0:T(8,128)}, f32[2048,512]{1,0:T(8,128)}, u32[]{:S(2)}, u32[]{:S(2)}) collective-permute-start(f32[2048,512]{1,0:T(8,128)} %slice.14), channel_id=1, source_target_pairs={{0,1},{2,3},{4,5},{6,7},{8,9},{10,11},{12,13},{14,15},{16,17},{18,... | collective-permute-start | bytes 12582920 | tf_op jit(solution)/shard_map/ppermute | solution.py:388
  48.5 31.4 %slice-start = ((s8[8388608]{0:T(1024)(128)(4,1)}), s8[4194304]{0:T(1024)(128)(4,1)S(1)}, s32[]{:S(2)}) async-start(s8[8388608]{0:T(1024)(128)(4,1)} %bitcast.7), calls=%async_computation | async-start | bytes 8388608
  50.6 29.3 %slice-start.1 = ((s8[8388608]{0:T(1024)(128)(4,1)}), s8[4194304]{0:T(1024)(128)(4,1)S(1)}, s32[]{:S(2)}) async-start(s8[8388608]{0:T(1024)(128)(4,1)} %bitcast.7), calls=%async_computation.1 | async-start | bytes 8388608
  50.7 55.2 %collective-permute-start.3 = (f32[1280,512]{1,0:T(8,128)S(1)}, f32[1280,512]{1,0:T(8,128)S(1)}, u32[]{:S(2)}, u32[]{:S(2)}) collective-permute-start(f32[1280,512]{1,0:T(8,128)S(1)} %slice.15), channel_id=1, source_target_pairs={{1,0},{3,2},{5,4},{7,6},{9,8},{11,10},{13,12},{15,14},{17,16},{19,... | collective-permute-start | bytes 7864328 | tf_op jit(solution)/shard_map/ppermute | solution.py:395
  82.3 121.7 %collective-permute-start.1 = (f32[2048,512]{1,0:T(8,128)}, f32[2048,512]{1,0:T(8,128)}, u32[]{:S(2)}, u32[]{:S(2)}) collective-permute-start(f32[2048,512]{1,0:T(8,128)} %slice.13), channel_id=1, source_target_pairs={{0,1},{2,3},{4,5},{6,7},{8,9},{10,11},{12,13},{14,15},{16,17},{18,... | collective-permute-start | bytes 12582920 | tf_op jit(solution)/shard_map/ppermute | solution.py:396
where the time goes:
time: 216 us; the launch traced here: 215 us
  Pallas kernels  181 us (84%)
  local copies, waits for them, and re-layouts  15.4 us (7%)
  starting transfers between devices  7.52 us (3%)
  matrix products  6.7 us (3%)
    pallas_call x3, Pallas kernels, talk(): pl.pallas_call(kernel, out_shape=jax.ShapeDtypeStruct(out_shape, jnp.floa...  101 us
    pallas_call x1, Pallas kernels, factor_second(): pl.pallas_call(second_kernel, out_shape=(square,) * 4, in_specs=[VMEM] *...  27.7 us
    pallas_call x2, Pallas kernels, basis_rows(): pl.pallas_call(functools.partial(basis_kernel, scale), out_shape=jax.Shap...  22.6 us
    pallas_call x1, Pallas kernels, factor_first(): pl.pallas_call(first_kernel, out_shape=(square, square), in_specs=[VMEM],...  20.3 us
    pallas_call x1, Pallas kernels, cross_gram(): pl.pallas_call(functools.partial(cross_kernel, early), out_shape=jax.Shap...  9.63 us
    dot_general x1, matrix products, on_device(): lax.dot_general(snapshots, snapshots, (((0,), (0,)), ((), ())), preferred...  6.7 us
    slice x1, local copies, waits for them, and re-layouts, on_device(): a1 = lax.ppermute(snapshots[:mid], 'snap', [(0, 1)])  5.29 us
  transfers between devices with their start and end apart: 4, of which 1 were waited for; matrix products, arithmetic and copies ran while one was open for 10% of the time, Pallas kernels for 79%

commit v1 on v0

--- a/solution.py
+++ b/solution.py
@@ -106,25 +106,6 @@
 VMEM = pl.BlockSpec(memory_space=pltpu.VMEM)
 
 
-def first_kernel(g_ref, l_ref, x_ref, a_ref):
-    a_ref[...] = g_ref[0]
-    factor_into(a_ref, l_ref, x_ref, g_ref.shape[1])
-
-
-def factor_first(grams):
-    n = grams.shape[1]
-    square = jax.ShapeDtypeStruct((n, n), jnp.float32)
-    return pl.pallas_call(
-        first_kernel,
-        out_shape=(square, square),
-        in_specs=[VMEM],
-        out_specs=(VMEM, VMEM),
-        scratch_shapes=[pltpu.VMEM((n, n), jnp.float32)],
-        compiler_params=pltpu.CompilerParams(vmem_limit_bytes=40 << 20),
-        cost_estimate=pl.CostEstimate(flops=24 << 30, bytes_accessed=80 << 20, transcendentals=0),
-    )(grams)
-
-
 def second_kernel(g_ref, c_ref, xa_ref, lba_ref, xba_ref, l_ref, x_ref, a_ref):
     n = xa_ref.shape[0]
     lba = dot_nt(c_ref[0], xa_ref[...])
@@ -195,7 +176,7 @@
     return pl.ds(pl.multiple_of(start, size), size)
 
 
-def scatter_sum(send, where, p_ref, half, quarter, piece, rc, rx, rz, ry):
+def scatter_sum(send, where, p_ref, half, quarter, rc, rx, rz, ry):
     over_core, over_x, over_z, down = where
     z, x, y, core = place()
     n = p_ref.shape[0]
@@ -231,108 +212,174 @@
     return rows(core * (n // 2) + x * (n // 8) + z * s, s)
 
 
-def scatter_kernel(p_ref, out_ref, half, quarter, piece, rc, rx, rz, ry, send_sem, recv_sem):
-    where = neighbours(True)
-    scatter_sum(Sender(send_sem, recv_sem), where, p_ref, half, quarter, piece, rc, rx, rz, ry)
-    out_ref[0] = ry[0] + ry[2]
-    out_ref[1] = ry[1] + ry[3]
-
-
-def gather_kernel(p_ref, out_ref, send_sem, recv_sem):
-    where = neighbours(False)
-    out_ref[:, own_rows(out_ref.shape[1]), :] = p_ref[...]
-    gather_rows(Sender(send_sem, recv_sem), where, out_ref)
-
-
-def reduce_kernel(p_ref, out_ref, half, quarter, piece, rc, rx, rz, ry, send_sem, recv_sem):
+def split(x):
+    high = x.astype(jnp.bfloat16)
+    return high, (x - high.astype(jnp.float32)).astype(jnp.bfloat16)
+
+
+def dot3(a, b, over):
+    dims = ((over[:1], over[1:]), ((), ()))
+    dot = lambda l, r: lax.dot_general(l, r, dims, preferred_element_type=jnp.float32)
+    return dot(a[0], b[0]) + (dot(a[0], b[1]) + dot(a[1], b[0]))
+
+
+CHUNK = 256
+HALF = CHUNK // 2
+PAIRED = 7
+EARLY = 2
+CROSS = 8 * CHUNK + HALF
+SENT = 11 * CHUNK
+
+
+def phase_kernel(x_ref, grams_ref, la_ref, xa_ref, cross_ref, got_ref, own, acc, half, quarter, rc, rx, rz, ry,
+                 half2, quarter2, rc2, rx2, rz2, ry2, load_sem, go_sem, come_sem, send_sem, recv_sem):
     where = neighbours(True)
     send = Sender(send_sem, recv_sem)
-    scatter_sum(send, where, p_ref, half, quarter, piece, rc, rx, rz, ry)
-    out_ref[0, own_rows(out_ref.shape[1]), :] = (ry[0] + ry[2]) + (ry[1] + ry[3])
-    gather_rows(send, where, out_ref)
-
-
-def scratch(n, copies):
+    snap = lax.axis_index("snap")
+    first, second = snap == 0, snap == 1
+    other = (lax.axis_index("dof"), 1 - snap)
+    count, n = x_ref.shape
+
+    def stream(c, base, size):
+        start = c * CHUNK if isinstance(c, int) else pl.multiple_of(c * CHUNK, CHUNK)
+        return pltpu.make_async_remote_copy(
+            src_ref=x_ref.at[pl.ds(base + start, size)], dst_ref=got_ref.at[pl.ds(start, size)],
+            send_sem=go_sem.at[c], recv_sem=come_sem.at[c], device_id=other, device_id_type=MESH)
+
+    def rest():
+        start = CROSS
+        return pltpu.make_async_remote_copy(
+            src_ref=x_ref.at[pl.ds(start, SENT - CROSS)], dst_ref=got_ref.at[pl.ds(start, SENT - CROSS)],
+            send_sem=go_sem.at[9], recv_sem=come_sem.at[9], device_id=other, device_id_type=MESH)
+
+    @pl.when(first)
+    def _():
+        for c in range(8):
+            stream(c, 0, CHUNK).start()
+        stream(8, 0, HALF).start()
+        rest().start()
+
+    @pl.when(second)
+    def _():
+        for c in range(EARLY):
+            stream(c, CROSS, CHUNK).start()
+
+    loads = count // CHUNK
+
+    def load(c):
+        at = pl.ds(pl.multiple_of(c * CHUNK, CHUNK), CHUNK)
+        return pltpu.make_async_copy(x_ref.at[at], own.at[at], load_sem.at[c])
+
+    def load_one(c, _):
+        load(c).start()
+        return 0
+
+    lax.fori_loop(0, loads, load_one, 0)
+    acc[...] = jnp.zeros_like(acc)
+
+    def gram_one(c, _):
+        load(c).wait()
+        high, low = split(own[pl.ds(pl.multiple_of(c * CHUNK, CHUNK), CHUNK), :])
+        acc[...] += dot_tn(high, high * jnp.bfloat16(0.5)) + dot_tn(high, low)
+        return 0
+
+    lax.fori_loop(0, loads, gram_one, 0)
+    acc[...] = acc[...] + acc[...].T
+
+    scatter_sum(send, where, acc, half, quarter, rc, rx, rz, ry)
+    mine = own_rows(n)
+    grams_ref[0, mine, :] = ry[0] + ry[2]
+    grams_ref[1, mine, :] = ry[1] + ry[3]
+
+    @pl.when(second)
+    def _():
+        for c in range(EARLY, PAIRED):
+            stream(c, CROSS, CHUNK).start()
+        stream(PAIRED, CROSS, HALF).start()
+
+    gather_rows(send, where, grams_ref)
+    acc[...] = grams_ref[0]
+    factor_into(acc, la_ref, xa_ref, n)
+
+    acc[...] = jnp.zeros_like(acc)
+
+    def add(start, size, own_start):
+        got = got_ref[pl.ds(start, size), :]
+        mine = own[pl.ds(own_start, size), :]
+        left = split(jnp.where(second, mine, got))
+        right = split(jnp.where(second, got, mine))
+        acc[...] += dot3(left, right, (0, 0))
+
+    def cross_one(c, _):
+        stream(c, 0, CHUNK).wait_recv()
+        start = pl.multiple_of(c * CHUNK, CHUNK)
+        add(start, CHUNK, pl.multiple_of(start + (1 - snap) * CROSS, HALF))
+        return 0
+
+    lax.fori_loop(0, PAIRED, cross_one, 0)
+
+    @pl.when(first)
+    def _():
+        stream(PAIRED, 0, HALF).wait_recv()
+        add(PAIRED * CHUNK, HALF, PAIRED * CHUNK + CROSS)
+
+    @pl.when(second)
+    def _():
+        stream(PAIRED, 0, CHUNK).wait_recv()
+        add(PAIRED * CHUNK, CHUNK, PAIRED * CHUNK)
+        stream(8, 0, HALF).wait_recv()
+        add(8 * CHUNK, HALF, 8 * CHUNK)
+
+    scatter_sum(send, where, acc, half2, quarter2, rc2, rx2, rz2, ry2)
+    cross_ref[0, mine, :] = (ry2[0] + ry2[2]) + (ry2[1] + ry2[3])
+    gather_rows(send, where, cross_ref)
+
+    @pl.when(first)
+    def _():
+        for c in range(8):
+            stream(c, 0, CHUNK).wait_send()
+        stream(8, 0, HALF).wait_send()
+        rest().wait_send()
+
+    @pl.when(second)
+    def _():
+        for c in range(PAIRED):
+            stream(c, CROSS, CHUNK).wait_send()
+        stream(PAIRED, CROSS, HALF).wait_send()
+        rest().wait_recv()
+
+
+def dot_tn(a, b):
+    return lax.dot_general(a, b, (((0,), (0,)), ((), ())), preferred_element_type=jnp.float32)
+
+
+def phase(snapshots):
+    count, n = snapshots.shape
     f32 = jnp.float32
-    return [
+    shape = lambda *s: jax.ShapeDtypeStruct(s, f32)
+    parts = [
         pltpu.VMEM((n // 2, n), f32),
         pltpu.VMEM((n // 8, n), f32),
-        pltpu.VMEM((n // 32, n), f32),
         pltpu.VMEM((n // 2, n), f32),
         pltpu.VMEM((3, n // 8, n), f32),
         pltpu.VMEM((3, n // 32, n), f32),
         pltpu.VMEM((4, n // 32, n), f32),
-        pltpu.SemaphoreType.DMA((copies,)),
-        pltpu.SemaphoreType.DMA((copies,)),
     ]
-
-
-def talk(kernel, out_shape, scratch_shapes, collective_id, operand):
+    dma = pltpu.SemaphoreType.DMA
     return pl.pallas_call(
-        kernel,
-        out_shape=jax.ShapeDtypeStruct(out_shape, jnp.float32),
-        in_specs=[VMEM],
-        out_specs=VMEM,
-        scratch_shapes=scratch_shapes,
+        phase_kernel,
+        out_shape=(shape(2, n, n), shape(n, n), shape(n, n), shape(1, n, n), shape(SENT, n)),
+        in_specs=[pl.BlockSpec(memory_space=pl.ANY)],
+        out_specs=(VMEM,) * 5,
+        scratch_shapes=[pltpu.VMEM((count, n), f32), pltpu.VMEM((n, n), f32)] + parts + parts
+        + [dma((count // CHUNK,)), dma((10,)), dma((10,)), dma((34,)), dma((34,))],
         compiler_params=pltpu.CompilerParams(
-            collective_id=collective_id, has_side_effects=True, vmem_limit_bytes=40 << 20),
-        cost_estimate=pl.CostEstimate(flops=32 << 30, bytes_accessed=100 << 20, transcendentals=0),
-    )(operand)
-
-
-def split(x):
-    high = x.astype(jnp.bfloat16)
-    return high, (x - high.astype(jnp.float32)).astype(jnp.bfloat16)
-
-
-def dot3(a, b, over):
-    dims = ((over[:1], over[1:]), ((), ()))
-    dot = lambda l, r: lax.dot_general(l, r, dims, preferred_element_type=jnp.float32)
-    return dot(a[0], b[0]) + (dot(a[0], b[1]) + dot(a[1], b[0]))
-
-
-CHUNK = 256
-
-
-def cross_kernel(early, who_ref, own_ref, a_ref, b1_ref, b2_ref, out_ref):
-    i = pl.program_id(0)
-    second = who_ref[0] == 1
-    got = jnp.where(second, a_ref[...], jnp.where(i < early, b1_ref[...], b2_ref[...]))
-    own = own_ref[...]
-    left = split(jnp.where(second, own, got))
-    right = split(jnp.where(second, got, own))
-
-    @pl.when(i == 0)
-    def _():
-        out_ref[...] = jnp.zeros_like(out_ref)
-
-    out_ref[...] += dot3(left, right, (0, 0))
-
-
-def cross_gram(snap, own, a, b1, b2):
-    steps, n = a.shape[0] // CHUNK, own.shape[1]
-    early, late = b1.shape[0] // CHUNK, b2.shape[0] // CHUNK
-    block = lambda index: pl.BlockSpec((CHUNK, n), index)
-    return pl.pallas_call(
-        functools.partial(cross_kernel, early),
-        out_shape=jax.ShapeDtypeStruct((n, n), jnp.float32),
-        grid_spec=pltpu.PrefetchScalarGridSpec(
-            num_scalar_prefetch=1,
-            grid=(steps,),
-            in_specs=[
-                block(lambda i, who: ((1 - who[0]) * steps + i, 0)),
-                block(lambda i, who: (who[0] * i, 0)),
-                block(lambda i, who: ((1 - who[0]) * jnp.minimum(i, early - 1), 0)),
-                block(lambda i, who: ((1 - who[0]) * jnp.clip(i - early, 0, late - 1), 0)),
-            ],
-            out_specs=pl.BlockSpec((n, n), lambda i, who: (0, 0)),
-        ),
-        compiler_params=pltpu.CompilerParams(vmem_limit_bytes=40 << 20),
-        cost_estimate=pl.CostEstimate(flops=3 << 30, bytes_accessed=12 << 20, transcendentals=0),
-    )(snap, own, a, b1, b2)
-
-
-TALL = 512
+            collective_id=0, has_side_effects=True, vmem_limit_bytes=56 << 20),
+        cost_estimate=pl.CostEstimate(flops=130 << 30, bytes_accessed=400 << 20, transcendentals=0),
+    )(snapshots)
+
+
+TALL = 256
 
 
 def basis_kernel(scale, who_ref, own_ref, a_ref, xa_ref, xb_ref, xba_ref, *others):
@@ -369,7 +416,7 @@
             scratch_shapes=[pltpu.VMEM((n, n), jnp.bfloat16)] * 4,
         ),
         input_output_aliases={6: 0} if extra else {},
-        compiler_params=pltpu.CompilerParams(vmem_limit_bytes=40 << 20),
+        compiler_params=pltpu.CompilerParams(vmem_limit_bytes=60 << 20),
         cost_estimate=pl.CostEstimate(flops=6 << 30, bytes_accessed=12 << 20, transcendentals=0),
     )(snap, own, a, xa, xb, xba, *extra)
 
@@ -379,35 +426,19 @@
     snap = lax.axis_index("snap")
     first = snap == 0
     who = snap.astype(jnp.int32).reshape(1)
-    rows_in_all = count * lax.axis_size("dof")
-    root_rows = float(rows_in_all) ** 0.5
-    mid = count // 2
-    early = mid + 3 * CHUNK
-
+    root_rows = float(count * lax.axis_size("dof")) ** 0.5
     tie = lambda *values: lax.optimization_barrier(values)
-    a1 = lax.ppermute(snapshots[:mid], "snap", [(0, 1)])
-    b1 = lax.ppermute(snapshots[mid:early], "snap", [(1, 0)])
-    own_gram = lax.dot_general(
-        snapshots, snapshots, (((0,), (0,)), ((), ())), preferred_element_type=jnp.float32, precision=lax.Precision.HIGH)
-    pieces = talk(scatter_kernel, (2, n // 32, n), scratch(n, 10), 0, own_gram)
-    b1, pieces = tie(b1, pieces)
-    late, pieces = tie(snapshots, pieces)
-    b2 = lax.ppermute(late[early:], "snap", [(1, 0)])
-    a2 = lax.ppermute(late[mid:], "snap", [(0, 1)])
-    grams = talk(gather_kernel, (2, n, n), scratch(n, 7)[-2:], 1, pieces)
-    la, xa = factor_first(grams)
-
-    a1, b1, b2, la = tie(a1, b1, b2, la)
-    cross = cross_gram(who, snapshots, a1, b1, b2)
-    cross = talk(reduce_kernel, (1, n, n), scratch(n, 17), 2, cross)
+
+    grams, la, xa, cross, a1 = phase(snapshots)
+    late, cross = tie(snapshots, cross)
+    a2 = lax.ppermute(late[SENT:], "snap", [(0, 1)])
     lba, xba, lb, xb = factor_second(grams, cross, xa)
-
-    basis = basis_rows(root_rows, 0, who, snapshots, a1, xa, xb, xba, None)
-    a2, basis = tie(a2, basis)
-    basis = basis_rows(root_rows, mid, who, snapshots, a2, xa, xb, xba, basis)
     top = jnp.where(first, la, lba).T
     bottom = jnp.where(first, 0.0, lb).T
     factor = jnp.concatenate([top, bottom]) / root_rows
+    basis = basis_rows(root_rows, 0, who, snapshots, a1, xa, xb, xba, None)
+    a2, basis, factor = tie(a2, basis, factor)
+    basis = basis_rows(root_rows, SENT, who, snapshots, a2, xa, xb, xba, basis)
     return (basis, factor)
 
 

time: 216 us -> 221 us (1.023)
  Pallas kernels: 181 us -> 199 us
  waiting for transfers between devices: 1.83 us -> 10.8 us
  local copies, waits for them, and re-layouts: 15.4 us -> 7.75 us
  matrix products: 6.7 us -> 0 us
  starting transfers between devices: 7.52 us -> 1.46 us
    pallas_call x5 -> x1, Pallas kernels: 131 us -> 143 us  [phase(): pl.pallas_call(phase_kernel, out_shape=(shape(2, n, n), shape(n, n), shap...]
    ppermute x4 -> x1, waiting for transfers between devices: 1.83 us -> 10.8 us  [on_device(): a2 = lax.ppermute(late[SENT:], 'snap', [(0, 1)])]
    slice x4 -> x1, local copies, waits for them, and re-layouts: 12.5 us -> 3.72 us  [on_device(): a2 = lax.ppermute(late[SENT:], 'snap', [(0, 1)])]
    dot_general x1 -> x0, matrix products: 6.7 us -> none  [on_device(): lax.dot_general(snapshots, snapshots, (((0,), (0,)), ((), ())), preferred...]
    ppermute x4 -> x1, starting transfers between devices: 7.52 us -> 1.46 us  [on_device(): a2 = lax.ppermute(late[SENT:], 'snap', [(0, 1)])]
    pallas_call x2, Pallas kernels: 22.6 us -> 27.9 us  [basis_rows(): pl.pallas_call(functools.partial(basis_kernel, scale), out_shape=jax.Shap...]
  transfers between devices with their start and end apart: 4 -> 1, of which waited for: 1 -> 1; matrix products, arithmetic and copies ran while one was open for 10% -> 0% of each run, Pallas kernels for 79% -> 21%
where the time goes in v1:
time: 221 us; the launch traced here: 220 us
  Pallas kernels  199 us (90%)
  waiting for transfers between devices  10.8 us (5%)
  local copies, waits for them, and re-layouts  7.75 us (4%)
    pallas_call x1, Pallas kernels, phase(): pl.pallas_call(phase_kernel, out_shape=(shape(2, n, n), shape(n, n), shap...  143 us
    pallas_call x2, Pallas kernels, basis_rows(): pl.pallas_call(functools.partial(basis_kernel, scale), out_shape=jax.Shap...  27.9 us
    pallas_call x1, Pallas kernels, factor_second(): pl.pallas_call(second_kernel, out_shape=(square,) * 4, in_specs=[VMEM] *...  27.5 us
    ppermute x1, waiting for transfers between devices, on_device(): a2 = lax.ppermute(late[SENT:], 'snap', [(0, 1)])  10.8 us
  transfers between devices with their start and end apart: 1, of which 1 were waited for; matrix products, arithmetic and copies ran while one was open for 0% of the time, Pallas kernels for 21%

profile of v1, /device:TPU:9, one launch (start us, length us, event | category | flops | bytes accessed | tf_op | source)
XLA Modules:
  0.0 220.1 jit_solution(18357164926985153978)
XLA Ops:
  0.6 143.4 %shard_map.30 = (f32[2,512,512]{2,1,0:T(8,128)}, f32[512,512]{1,0:T(8,128)}, f32[512,512]{1,0:T(8,128)}, f32[1,512,512]{2,1,0:T(8,128)}, f32[2816,512]{1,0:T(8,128)}) custom-call(f32[4096,512]{1,0:T(8,128)} %own_ref.3), custom_call_target="tpu_custom_call" | custom-call | flops 139586437120 | bytes 419430400 | tf_op jit(solution)/shard_map/pallas_call | solution.py:369
  144.1 0.0 copy-start
  144.1 0.0 copy-start.3
  144.1 3.7 %slice.3 = f32[1280,512]{1,0:T(8,128)} slice(f32[4096,512]{1,0:T(8,128)} %own_ref.3), slice={[2816:4096], [0:512]} | slice | bytes 5242880 | tf_op jit(solution)/shard_map/slice | solution.py:434
  147.8 1.5 collective-permute-start
  149.3 0.0 copy-done
  149.3 0.0 copy-done.3
  149.3 0.0 copy-start.4
  149.3 1.2 copy-done.4
  150.5 0.0 copy-start.5
  150.5 27.5 %shard_map.31 = (f32[512,512]{1,0:T(8,128)S(1)}, f32[512,512]{1,0:T(8,128)S(1)}, f32[512,512]{1,0:T(8,128)S(1)}, f32[512,512]{1,0:T(8,128)S(1)}) custom-call(f32[2,512,512]{2,1,0:T(8,128)S(1)} %copy-done.3, f32[1,512,512]{2,1,0:T(8,128)S(1)} %copy-done.4, f32[512,512]{1,0:T(8,128)S(1)} %copy-done), custom_call_target="tpu_custom_call" | custom-call | flops 25769803776 | bytes 83886080 | tf_op jit(solution)/shard_map/pallas_call | solution.py:121
  178.0 0.0 copy-start.1
  178.0 0.0 copy-start.2
  178.0 0.0 copy-done.5
  178.0 0.4 select_bitcast_fusion
  178.4 0.6 copy-done.1
  179.0 0.4 copy-done.2
  179.4 0.2 maximum_multiply_fusion
  179.6 17.9 %shard_map.32.others_0_ = f32[4096,512]{1,0:T(8,128)} custom-call(s32[1]{0:T(128)} %bitcast.who_ref, f32[4096,512]{1,0:T(8,128)} %own_ref.3, f32[2816,512]{1,0:T(8,128)} %get-tuple-element.18.a_ref, f32[512,512]{1,0:T(8,128)} %get-tuple-element.19.xa_ref, f32[512,512]{1,0:T(8,128)} %copy-done.2, f32[512,512]{1,0:T(8,128)} %copy-done.1), custom_call_target="tpu_custom_call" | custom-call | flops 6442450944 | bytes 12582912 | tf_op jit(solution)/shard_map/pallas_call | solution.py:407
  197.5 10.8 %collective-permute-done.a_ref = f32[1280,512]{1,0:T(8,128)} collective-permute-done((f32[1280,512]{1,0:T(8,128)}, f32[1280,512]{1,0:T(8,128)}, u32[]{:S(2)}, u32[]{:S(2)}) %collective-permute-start) | collective-permute-done | bytes 2621472 | tf_op jit(solution)/shard_map/ppermute | solution.py:434
  208.3 1.8 copy.4
  210.1 10.0 %shard_map.33 = f32[4096,512]{1,0:T(8,128)} custom-call(s32[1]{0:T(128)} %bitcast.who_ref, f32[4096,512]{1,0:T(8,128)} %own_ref.3, f32[1280,512]{1,0:T(8,128)} %collective-permute-done.a_ref, f32[512,512]{1,0:T(8,128)} %get-tuple-element.19.xa_ref, f32[512,512]{1,0:T(8,128)} %copy-done.2, f32[512,512]{1,0:T(8,128)} %copy-done.1, ...), custom_call_target="tpu_custom_call", output_to_operand_aliasing={{}: (6, {})} | custom-call | flops 6442450944 | bytes 12582912 | tf_op jit(solution)/shard_map/pallas_call | solution.py:407
Async XLA Ops:
  144.1 5.2 %copy-start = (f32[512,512]{1,0:T(8,128)S(1)}, f32[512,512]{1,0:T(8,128)}, u32[]{:S(2)}) copy-start(f32[512,512]{1,0:T(8,128)} %get-tuple-element.19.xa_ref) | copy-start | bytes 3145732
  144.1 5.2 %copy-start.3 = (f32[2,512,512]{2,1,0:T(8,128)S(1)}, f32[2,512,512]{2,1,0:T(8,128)}, u32[]{:S(2)}) copy-start(f32[2,512,512]{2,1,0:T(8,128)} %get-tuple-element.20.g_ref) | copy-start | bytes 6291460
  147.8 60.5 %collective-permute-start = (f32[1280,512]{1,0:T(8,128)}, f32[1280,512]{1,0:T(8,128)}, u32[]{:S(2)}, u32[]{:S(2)}) collective-permute-start(f32[1280,512]{1,0:T(8,128)} %slice.3), channel_id=1, source_target_pairs={{0,1},{2,3},{4,5},{6,7},{8,9},{10,11},{12,13},{14,15},{16,17},{18,... | collective-permute-start | bytes 7864328 | tf_op jit(solution)/shard_map/ppermute | solution.py:434
  149.3 1.2 copy-start.4
  150.5 27.5 %copy-start.5 = (f32[512,512]{1,0:T(8,128)S(1)}, f32[512,512]{1,0:T(8,128)}, u32[]{:S(2)}) copy-start(f32[512,512]{1,0:T(8,128)} %get-tuple-element.24) | copy-start | bytes 3145732
  178.0 1.0 copy-start.1
  178.0 1.4 copy-start.2

commit v2 on v1

v2 whole, which is shorter than its diff:
```python
import functools

import jax
import jax.numpy as jnp
from jax import lax
from jax.experimental import pallas as pl
from jax.experimental.pallas import tpu as pltpu
from jax.sharding import PartitionSpec as P

MESH = pl.DeviceIdType.MESH
HI = lax.Precision.HIGHEST
T = 128

def dot_nt(a, b):
    return lax.dot_general(a, b, (((1,), (1,)), ((), ())), preferred_element_type=jnp.float32, precision=HI)

def dot_nn(a, b):
    return lax.dot_general(a, b, (((1,), (0,)), ((), ())), preferred_element_type=jnp.float32, precision=HI)

def eliminate(block):
    sub = lax.broadcasted_iota(jnp.int32, (8, T), 0)
    lane = lax.broadcasted_iota(jnp.int32, (8, T), 1)
    rows = [block[8 * i:8 * i + 8, :] for i in range(T // 8)]
    upper, lower, pivots = [], [], []
    for b in range(T // 8):
        first = 8 * b
        in_block = (lane >= first) & (lane < first + 8)
        head = rows[b]
        cols = [jnp.broadcast_to(head[:, first + k:first + k + 1], (8, T)) for k in range(8)]
        t = {}
        for k in range(8):
            for j in range(k + 1):
                t[j, k] = jnp.broadcast_to(cols[k][j:j + 1, :], (8, T))
        recip = []
        for j in range(8):
            r = 1.0 / t[j, j]
            recip.append(r)
            for k in range(j + 1, 8):
                s = t[j, k] * r
                for l in range(k, 8):
                    t[k, l] = t[k, l] - s * t[j, l]
        pivot = t[0, 0]
        for j in range(1, 8):
            pivot = jnp.where(sub == j, t[j, j], pivot)
        pivots.append(pivot)

        def multipliers(cs, below):
            cs = list(cs)
            out = []
            for j in range(8):
                m = cs[j] * recip[j]
                if not below:
                    m = jnp.where(sub > j, m, 0.0)
                out.append(m)
                for k in range(j + 1, 8):
                    cs[k] = cs[k] - m * t[j, k]
            return out

        v = jnp.where(in_block, jnp.where(lane == sub + first, 1.0, 0.0), head)
        m = multipliers(cols, False)
        own = head
        for j in range(8):
            v = v - m[j] * jnp.broadcast_to(v[j:j + 1, :], (8, T))
            own = own - m[j] * jnp.broadcast_to(own[j:j + 1, :], (8, T))
        vb = [jnp.broadcast_to(v[j:j + 1, :], (8, T)) for j in range(8)]
        upper.append(jnp.where(lane >= sub + first, own, 0.0))
        lower.append(jnp.where(lane <= sub + first, v, 0.0))
        for i in range(b + 1, T // 8):
            cs = [jnp.broadcast_to(rows[i][:, first + k:first + k + 1], (8, T)) for k in range(8)]
            m = multipliers(cs, True)
            w = jnp.where(in_block, 0.0, rows[i])
            for j in range(8):
                w = w - m[j] * vb[j]
            rows[i] = w
    cat = lambda x: jnp.concatenate(x, axis=0)
    return cat(lower), cat(upper), cat(pivots)

def factor_into(a_ref, l_ref, x_ref, n, lt_ref=None):
    steps = n // T
    def step(p, _):
        at = pl.ds(pl.multiple_of(p * T, T), T)
        low, up, piv = eliminate(a_ref[at, at])
        scale = lax.rsqrt(piv)
        xd = low * scale
        ld = up * scale
        x_ref[at, at] = xd
        l_ref[at, at] = ld.T
        for k in range(steps):
            @pl.when(p == k)
            def _():
                o = k * T
                e = o + T
                if k > 0:
                    part = dot_nn(l_ref[o:e, 0:o], x_ref[0:o, 0:o])
                    x_ref[o:e, 0:o] = -dot_nn(xd, part)
                if e < n:
                    x_ref[o:e, e:n] = jnp.zeros((T, n - e), jnp.float32)
                    l_ref[o:e, e:n] = jnp.zeros((T, n - e), jnp.float32)
                    l21 = dot_nt(a_ref[e:n, o:e], xd)
                    l_ref[e:n, o:e] = l21
                    a_ref[e:n, e:n] = a_ref[e:n, e:n] - dot_nt(l21, l21)
        return 0
    lax.fori_loop(0, steps, step, 0)


VMEM = pl.BlockSpec(memory_space=pltpu.VMEM)


def place():
    dof, snap = lax.axis_index("dof"), lax.axis_index("snap")
    core, y_hi = lax.rem(dof, 2), lax.rem(dof // 2, 2)
    return dof // 16, lax.rem(dof // 4, 4), y_hi * 2 + snap, core


def device(z, x, y, core):
    return (z * 16 + x * 4 + (y // 2) * 2 + core, lax.rem(y, 2))


def neighbours(with_y):
    z, x, y, core = place()
    over_core = [device(z, x, y, 1 - core)]
    over_x = [device(z, lax.rem(x + k, 4), y, core) for k in (1, 2, 3)]
    over_z = [device(lax.rem(z + k, 4), x, y, core) for k in (1, 2, 3)]
    down = device(z, x, lax.rem(y + 3, 4), core)
    greet = over_core + over_x + over_z
    if with_y:
        greet = greet + [down, device(z, x, lax.rem(y + 1, 4), core)]
    barrier = pltpu.get_barrier_semaphore()
    for partner in greet:
        pl.semaphore_signal(barrier, inc=1, device_id=partner, device_id_type=MESH)
    pl.semaphore_wait(barrier, len(greet))
    return over_core, over_x, over_z, down


class Sender:
    def __init__(self, send_sem, recv_sem):
        self.sems, self.used = (send_sem, recv_sem), 0

    def start(self, src, dst, to):
        send_sem, recv_sem = (s.at[self.used] for s in self.sems)
        self.used += 1
        copy = pltpu.make_async_remote_copy(
            src_ref=src, dst_ref=dst, send_sem=send_sem, recv_sem=recv_sem, device_id=to, device_id_type=MESH)
        copy.start()
        return copy

    def run(self, triples):
        for copy in [self.start(*t) for t in triples]:
            copy.wait()


def rows(start, size):
    return pl.ds(pl.multiple_of(start, size), size)


def scatter_sum(send, where, p_ref, half, quarter, rc, r1, r2, ry):
    over_core, over_x, over_z, down = where
    z, x, y, core = place()
    n = p_ref.shape[0]
    h, q, s, w = n // 2, n // 8, n // 32, n // 2
    left, right = pl.ds(0, w), pl.ds(w, w)
    send.run([(p_ref.at[rows((1 - core) * h, h)], rc, over_core[0])])
    half[...] = p_ref[rows(core * h, h), :] + rc[...]
    jobs = []
    for k in (2, 1, 3):
        jobs.append((half.at[rows(lax.rem(x + k, 4) * q, q), left], r1.at[0, k - 1], over_x[k - 1]))
        jobs.append((half.at[rows(lax.rem(z + k, 4) * q, q), right], r1.at[1, k - 1], over_z[k - 1]))
    send.run(jobs)
    quarter[0] = (half[rows(x * q, q), left] + r1[0, 1]) + (r1[0, 0] + r1[0, 2])
    quarter[1] = (half[rows(z * q, q), right] + r1[1, 1]) + (r1[1, 0] + r1[1, 2])
    jobs = []
    for k in (2, 1, 3):
        jobs.append((quarter.at[0, rows(lax.rem(z + k, 4) * s, s)], r2.at[0, k - 1], over_z[k - 1]))
        jobs.append((quarter.at[1, rows(lax.rem(x + k, 4) * s, s)], r2.at[1, k - 1], over_x[k - 1]))
    send.run(jobs)
    ry[y, 0] = (quarter[0, rows(z * s, s), :] + r2[0, 1]) + (r2[0, 0] + r2[0, 2])
    ry[y, 1] = (quarter[1, rows(x * s, s), :] + r2[1, 1]) + (r2[1, 0] + r2[1, 2])
    for k in (0, 1, 2):
        slot = ry.at[lax.rem(y + k, 4)]
        send.run([(slot, slot, down)])


def put_piece(out_ref, block, ry, slots):
    z, x, y, core = place()
    n = out_ref.shape[1]
    h, q, s, w = n // 2, n // 8, n // 32, n // 2
    at = (core * h + x * q + z * s, core * h + z * q + x * s)
    for side in (0, 1):
        total = ry[slots[0], side] + ry[slots[1], side]
        for i in range(2, len(slots), 2):
            total = total + (ry[slots[i], side] + ry[slots[i + 1], side])
        out_ref[block, rows(at[side], s), pl.ds(side * w, w)] = total


def gather_rows(send, where, out_ref):
    over_core, over_x, over_z, down = where
    z, x, y, core = place()
    n = out_ref.shape[1]
    h, q, s, w = n // 2, n // 8, n // 32, n // 2
    left, right = pl.ds(0, w), pl.ds(w, w)
    lpart = out_ref.at[:, rows(core * h + x * q + z * s, s), left]
    rpart = out_ref.at[:, rows(core * h + z * q + x * s, s), right]
    jobs = []
    for k in (2, 1, 3):
        jobs += [(lpart, lpart, over_z[k - 1]), (rpart, rpart, over_x[k - 1])]
    send.run(jobs)
    lpart = out_ref.at[:, rows(core * h + x * q, q), left]
    rpart = out_ref.at[:, rows(core * h + z * q, q), right]
    jobs = []
    for k in (2, 1, 3):
        jobs += [(lpart, lpart, over_x[k - 1]), (rpart, rpart, over_z[k - 1])]
    send.run(jobs)
    part = out_ref.at[:, rows(core * h, h)]
    send.run([(part, part, over_core[0])])


def split(x):
    high = x.astype(jnp.bfloat16)
    return high, (x - high.astype(jnp.float32)).astype(jnp.bfloat16)


def dot3(a, b, over):
    dims = ((over[:1], over[1:]), ((), ()))
    dot = lambda l, r: lax.dot_general(l, r, dims, preferred_element_type=jnp.float32)
    return dot(a[0], b[0]) + (dot(a[0], b[1]) + dot(a[1], b[0]))


CHUNK = 256
EARLY = 2


def dot_tn(a, b):
    return lax.dot_general(a, b, (((0,), (0,)), ((), ())), preferred_element_type=jnp.float32)


def thrice(x):
    high, low = split(x)
    return [high, high, low]


def weights(x):
    high, low = split(x)
    return jnp.concatenate([high, low, high], axis=1)


def whole_kernel(root, x_ref, own, factor_ref, got, grams, la, xa, cross, lba, lb, xb, xba, acc, w,
                 half, quarter, rc, r1, r2, ry, half_b, quarter_b, rc_b, r1_b, r2_b, ry_b,
                 load_sem, go_sem, come_sem, send_sem, recv_sem):
    where = neighbours(True)
    send = Sender(send_sem, recv_sem)
    snap = lax.axis_index("snap")
    first, second = snap == 0, snap == 1
    other = (lax.axis_index("dof"), 1 - snap)
    count, n = x_ref.shape
    chunks = count // CHUNK
    paired = chunks // 2
    chunk = lambda c: pl.ds(pl.multiple_of(c * CHUNK, CHUNK), CHUNK)

    def stream(c, ahead):
        return pltpu.make_async_remote_copy(
            src_ref=x_ref.at[chunk(c + ahead)], dst_ref=got.at[chunk(c)],
            send_sem=go_sem.at[c], recv_sem=come_sem.at[c], device_id=other, device_id_type=MESH)

    def loop(begin, end, body):
        def step(c, carry):
            body(c)
            return carry

        lax.fori_loop(begin, end, step, 0)

    @pl.when(first)
    def _():
        loop(0, chunks, lambda c: stream(c, 0).start())

    @pl.when(second)
    def _():
        loop(0, EARLY, lambda c: stream(c, paired).start())

    load = lambda c: pltpu.make_async_copy(x_ref.at[chunk(c)], own.at[chunk(c)], load_sem.at[c])
    loop(0, chunks, lambda c: load(c).start())
    acc[...] = jnp.zeros_like(acc)

    def gram_one(c):
        load(c).wait()
        high, low = split(own[chunk(c), :])
        acc[...] += dot_tn(high, high * jnp.bfloat16(0.5)) + dot_tn(high, low)

    loop(0, chunks, gram_one)
    acc[...] = acc[...] + acc[...].T

    scatter_sum(send, where, acc, half, quarter, rc, r1, r2, ry)
    put_piece(grams, 0, ry, (0, 2))
    put_piece(grams, 1, ry, (1, 3))

    @pl.when(second)
    def _():
        loop(EARLY, paired, lambda c: stream(c, paired).start())

    gather_rows(send, where, grams)
    acc[...] = grams[0]
    factor_into(acc, la, xa, n)

    def basis_one(c, values, width):
        own[chunk(c), :] = lax.dot_general(
            jnp.concatenate(values, axis=1), w[:, :width], (((1,), (1,)), ((), ())),
            preferred_element_type=jnp.float32)

    @pl.when(first)
    def _():
        w[:, :3 * n] = weights(xa[...] * root)
        factor_ref[:n, :] = la[...].T / root
        factor_ref[n:, :] = jnp.zeros((n, n), jnp.float32)

    acc[...] = jnp.zeros_like(acc)

    def cross_one(c):
        stream(c, 0).wait_recv()
        there = got[chunk(c), :]
        here = own[chunk(c + (1 - snap) * paired), :]
        left = split(jnp.where(second, here, there))
        right = split(jnp.where(second, there, here))
        acc[...] += dot3(left, right, (0, 0))

    loop(0, paired, cross_one)
    scatter_sum(send, where, acc, half_b, quarter_b, rc_b, r1_b, r2_b, ry_b)
    put_piece(cross, 0, ry_b, (0, 2, 1, 3))
    gather_rows(send, where, cross)

    @pl.when(second)
    def _():
        lba[...] = dot_nt(cross[0], xa[...])
        acc[...] = grams[1] - dot_nt(lba[...], lba[...])
        factor_into(acc, lb, xb, n)
        xba[...] = -dot_nn(xb[...], dot_nn(lba[...], xa[...]))
        w[:, :3 * n] = weights(xb[...] * root)
        w[:, 3 * n:] = weights(xba[...] * root)
        factor_ref[:n, :] = lba[...].T / root
        factor_ref[n:, :] = lb[...].T / root

        def one(c):
            @pl.when(c >= paired)
            def _():
                stream(c, 0).wait_recv()

            basis_one(c, thrice(own[chunk(c), :]) + thrice(got[chunk(c), :]), 6 * n)

        loop(0, chunks, one)
        loop(0, paired, lambda c: stream(c, paired).wait_send())

    @pl.when(first)
    def _():
        loop(0, chunks, lambda c: basis_one(c, thrice(own[chunk(c), :]), 3 * n))
        loop(0, chunks, lambda c: stream(c, 0).wait_send())


def whole(snapshots, root):
    count, n = snapshots.shape
    chunks = count // CHUNK
    f32 = jnp.float32
    sums = [
        pltpu.VMEM((n // 2, n), f32),
        pltpu.VMEM((2, n // 8, n // 2), f32),
        pltpu.VMEM((n // 2, n), f32),
        pltpu.VMEM((2, 3, n // 8, n // 2), f32),
        pltpu.VMEM((2, 3, n // 32, n // 2), f32),
        pltpu.VMEM((4, 2, n // 32, n // 2), f32),
    ]
    square = pltpu.VMEM((n, n), f32)
    dma = pltpu.SemaphoreType.DMA
    return pl.pallas_call(
        functools.partial(whole_kernel, root),
        out_shape=(jax.ShapeDtypeStruct((count, n), f32), jax.ShapeDtypeStruct((2 * n, n), f32)),
        in_specs=[pl.BlockSpec(memory_space=pl.ANY)],
        out_specs=(VMEM, VMEM),
        scratch_shapes=[pltpu.VMEM((count, n), f32)]
        + [pltpu.VMEM((2, n, n), f32), square, square, pltpu.VMEM((1, n, n), f32)] + [square] * 5
        + [pltpu.VMEM((n, 6 * n), jnp.bfloat16)] + sums + sums
        + [dma((chunks,)), dma((chunks,)), dma((chunks,)), dma((58,)), dma((58,))],
        compiler_params=pltpu.CompilerParams(
            collective_id=0, has_side_effects=True, vmem_limit_bytes=40 << 20),
        cost_estimate=pl.CostEstimate(flops=130 << 30, bytes_accessed=400 << 20, transcendentals=0),
    )(snapshots)


def on_device(snapshots):
    root_rows = float(snapshots.shape[0] * lax.axis_size("dof")) ** 0.5
    return tuple(whole(snapshots, root_rows))


def solution(mesh):
    in_specs = (P("dof", "snap"),)
    out_specs = (P("dof", "snap"), P(None, "snap"))
    return jax.shard_map(
        on_device, mesh=mesh, in_specs=in_specs, out_specs=out_specs, check_vma=False
    )
```

time: 221 us -> 194 us (0.88)
  Pallas kernels: 199 us -> 187 us
  waiting for transfers between devices: 10.8 us -> 0 us
  local copies, waits for them, and re-layouts: 7.75 us -> 4.72 us
    pallas_call x4 -> x1, Pallas kernels: 199 us -> 187 us  [whole(): pl.pallas_call(functools.partial(whole_kernel, root), out_shape=(jax.Shap...]
    ppermute x1 -> x0, waiting for transfers between devices: 10.8 us -> none  [on_device(): a2 = lax.ppermute(late[SENT:], 'snap', [(0, 1)])]
    slice x1 -> x0, local copies, waits for them, and re-layouts: 3.72 us -> none  [on_device(): a2 = lax.ppermute(late[SENT:], 'snap', [(0, 1)])]
    unnamed x13 -> x2, local copies, waits for them, and re-layouts: 4.03 us -> 4.72 us
  transfers between devices with their start and end apart: 1 -> 0, of which waited for: 1 -> 0; matrix products, arithmetic and copies ran while one was open for 0% -> 0% of each run, Pallas kernels for 21% -> 0%
where the time goes in v2:
time: 194 us; the launch traced here: 192 us
  Pallas kernels  187 us (96%)
  local copies, waits for them, and re-layouts  4.72 us (2%)
    pallas_call x1, Pallas kernels, whole(): pl.pallas_call(functools.partial(whole_kernel, root), out_shape=(jax.Shap...  187 us
    unnamed x2, local copies, waits for them, and re-layouts  4.72 us

profile of v2, /device:TPU:9, one launch (start us, length us, event | category | flops | bytes accessed | tf_op | source)
XLA Modules:
  0.0 192.3 jit_solution(10912961063826671298)
XLA Ops:
  0.6 186.9 %shard_map.30 = (f32[4096,512]{1,0:T(8,128)S(1)}, f32[1024,512]{1,0:T(8,128)S(1)}) custom-call(f32[4096,512]{1,0:T(8,128)} %x_ref.1), custom_call_target="tpu_custom_call" | custom-call | flops 139586437120 | bytes 419430400 | tf_op jit(solution)/shard_map/pallas_call | solution.py:370
  187.5 3.4 %copy.5 = f32[4096,512]{1,0:T(8,128)} copy(f32[4096,512]{1,0:T(8,128)S(1)} %get-tuple-element.4) | data formatting | bytes 16777216
  190.9 1.3 copy.6

commit v3 on v2

--- a/solution.py
+++ b/solution.py
@@ -227,6 +227,7 @@
 
 CHUNK = 256
 EARLY = 2
+ROUND = 2
 
 
 def dot_tn(a, b):
@@ -243,10 +244,9 @@
     return jnp.concatenate([high, low, high], axis=1)
 
 
-def whole_kernel(root, x_ref, own, factor_ref, got, grams, la, xa, cross, lba, lb, xb, xba, acc, w,
+def whole_kernel(root, x_ref, own, factor_ref, got, relay, grams, la, xa, cross, lba, lb, xb, xba, acc, w,
                  half, quarter, rc, r1, r2, ry, half_b, quarter_b, rc_b, r1_b, r2_b, ry_b,
-                 load_sem, go_sem, come_sem, send_sem, recv_sem):
-    where = neighbours(True)
+                 load_sem, go_sem, come_sem, hop_go_sem, hop_come_sem, send_sem, recv_sem):
     send = Sender(send_sem, recv_sem)
     snap = lax.axis_index("snap")
     first, second = snap == 0, snap == 1
@@ -254,7 +254,9 @@
     count, n = x_ref.shape
     chunks = count // CHUNK
     paired = chunks // 2
+    direct = chunks - ROUND
     chunk = lambda c: pl.ds(pl.multiple_of(c * CHUNK, CHUNK), CHUNK)
+    pair = lambda c: pl.ds(pl.multiple_of(c * 2 * CHUNK, 2 * CHUNK), 2 * CHUNK)
 
     def stream(c, ahead):
         return pltpu.make_async_remote_copy(
@@ -268,16 +270,27 @@
 
         lax.fori_loop(begin, end, step, 0)
 
-    @pl.when(first)
-    def _():
-        loop(0, chunks, lambda c: stream(c, 0).start())
-
-    @pl.when(second)
-    def _():
-        loop(0, EARLY, lambda c: stream(c, paired).start())
-
     load = lambda c: pltpu.make_async_copy(x_ref.at[chunk(c)], own.at[chunk(c)], load_sem.at[c])
     loop(0, chunks, lambda c: load(c).start())
+    where = neighbours(True)
+    down = where[3]
+
+    def hop(which, i):
+        src = (x_ref.at[chunk(direct + i)], relay.at[i], relay.at[i])[which]
+        dst = (relay.at[i], relay.at[i], got.at[chunk(direct + i)])[which]
+        go = hop_go_sem.at[i if which < 2 else ROUND + i]
+        come = hop_come_sem.at[i] if which < 2 else come_sem.at[direct + i]
+        return pltpu.make_async_remote_copy(
+            src_ref=src, dst_ref=dst, send_sem=go, recv_sem=come, device_id=down, device_id_type=MESH)
+
+    @pl.when(first)
+    def _():
+        loop(0, direct, lambda c: stream(c, 0).start())
+
+    @pl.when(second)
+    def _():
+        loop(0, EARLY, lambda c: stream(c, paired).start())
+
     acc[...] = jnp.zeros_like(acc)
 
     def gram_one(c):
@@ -296,12 +309,17 @@
     def _():
         loop(EARLY, paired, lambda c: stream(c, paired).start())
 
+    @pl.when(first)
+    def _():
+        for i in range(ROUND):
+            hop(0, i).start()
+
     gather_rows(send, where, grams)
     acc[...] = grams[0]
     factor_into(acc, la, xa, n)
 
     def basis_one(c, values, width):
-        own[chunk(c), :] = lax.dot_general(
+        own[pair(c), :] = lax.dot_general(
             jnp.concatenate(values, axis=1), w[:, :width], (((1,), (1,)), ((), ())),
             preferred_element_type=jnp.float32)
 
@@ -321,10 +339,33 @@
         right = split(jnp.where(second, there, here))
         acc[...] += dot3(left, right, (0, 0))
 
+    @pl.when(second)
+    def _():
+        hop(0, 0).wait_recv()
+        hop(1, 0).start()
+
     loop(0, paired, cross_one)
     scatter_sum(send, where, acc, half_b, quarter_b, rc_b, r1_b, r2_b, ry_b)
     put_piece(cross, 0, ry_b, (0, 2, 1, 3))
+
+    @pl.when(second)
+    def _():
+        for i in range(1, ROUND):
+            hop(0, i).wait_recv()
+            hop(1, i).start()
+
+    @pl.when(first)
+    def _():
+        hop(1, 0).wait_recv()
+        hop(2, 0).start()
+
     gather_rows(send, where, cross)
+
+    @pl.when(first)
+    def _():
+        for i in range(1, ROUND):
+            hop(1, i).wait_recv()
+            hop(2, i).start()
 
     @pl.when(second)
     def _():
@@ -338,19 +379,25 @@
         factor_ref[n:, :] = lb[...].T / root
 
         def one(c):
-            @pl.when(c >= paired)
+            @pl.when(c >= paired // 2)
             def _():
-                stream(c, 0).wait_recv()
-
-            basis_one(c, thrice(own[chunk(c), :]) + thrice(got[chunk(c), :]), 6 * n)
-
-        loop(0, chunks, one)
+                stream(2 * c, 0).wait_recv()
+                stream(2 * c + 1, 0).wait_recv()
+
+            basis_one(c, thrice(own[pair(c), :]) + thrice(got[pair(c), :]), 6 * n)
+
+        loop(0, paired, one)
         loop(0, paired, lambda c: stream(c, paired).wait_send())
-
-    @pl.when(first)
-    def _():
-        loop(0, chunks, lambda c: basis_one(c, thrice(own[chunk(c), :]), 3 * n))
-        loop(0, chunks, lambda c: stream(c, 0).wait_send())
+        for i in range(ROUND):
+            hop(1, i).wait_send()
+
+    @pl.when(first)
+    def _():
+        loop(0, paired, lambda c: basis_one(c, thrice(own[pair(c), :]), 3 * n))
+        loop(0, direct, lambda c: stream(c, 0).wait_send())
+        for i in range(ROUND):
+            hop(0, i).wait_send()
+            hop(2, i).wait_send()
 
 
 def whole(snapshots, root):
@@ -372,10 +419,10 @@
         out_shape=(jax.ShapeDtypeStruct((count, n), f32), jax.ShapeDtypeStruct((2 * n, n), f32)),
         in_specs=[pl.BlockSpec(memory_space=pl.ANY)],
         out_specs=(VMEM, VMEM),
-        scratch_shapes=[pltpu.VMEM((count, n), f32)]
+        scratch_shapes=[pltpu.VMEM((count, n), f32), pltpu.VMEM((ROUND, CHUNK, n), f32)]
         + [pltpu.VMEM((2, n, n), f32), square, square, pltpu.VMEM((1, n, n), f32)] + [square] * 5
         + [pltpu.VMEM((n, 6 * n), jnp.bfloat16)] + sums + sums
-        + [dma((chunks,)), dma((chunks,)), dma((chunks,)), dma((58,)), dma((58,))],
+        + [dma((chunks,)), dma((chunks,)), dma((chunks,)), dma((2 * ROUND,)), dma((ROUND,)), dma((58,)), dma((58,))],
         compiler_params=pltpu.CompilerParams(
             collective_id=0, has_side_effects=True, vmem_limit_bytes=40 << 20),
         cost_estimate=pl.CostEstimate(flops=130 << 30, bytes_accessed=400 << 20, transcendentals=0),

time: 194 us -> 188 us (0.969)
  Pallas kernels: 187 us -> 182 us
    pallas_call x1, Pallas kernels: 187 us -> 182 us  [whole(): pl.pallas_call(functools.partial(whole_kernel, root), out_shape=(jax.Shap...]
where the time goes in v3:
time: 188 us
  Pallas kernels  182 us (97%)
  local copies, waits for them, and re-layouts  4.72 us (3%)
    pallas_call x1, Pallas kernels, whole(): pl.pallas_call(functools.partial(whole_kernel, root), out_shape=(jax.Shap...  182 us
    unnamed x2, local copies, waits for them, and re-layouts  4.72 us

profile of v3, /device:TPU:9, one launch (start us, length us, event | category | flops | bytes accessed | tf_op | source)
XLA Modules:
  0.0 187.7 jit_solution(13282065710469472239)
XLA Ops:
  0.6 182.3 %shard_map.30 = (f32[4096,512]{1,0:T(8,128)S(1)}, f32[1024,512]{1,0:T(8,128)S(1)}) custom-call(f32[4096,512]{1,0:T(8,128)} %x_ref.1), custom_call_target="tpu_custom_call" | custom-call | flops 139586437120 | bytes 419430400 | tf_op jit(solution)/shard_map/pallas_call | solution.py:417
  182.9 3.4 %copy.5 = f32[4096,512]{1,0:T(8,128)} copy(f32[4096,512]{1,0:T(8,128)S(1)} %get-tuple-element.4) | data formatting | bytes 16777216
  186.3 1.3 copy.6

commit v4 on v3

--- a/solution.py
+++ b/solution.py
@@ -227,6 +227,9 @@
 
 CHUNK = 256
 EARLY = 2
+HALF = CHUNK // 2
+CROSS = 8 * CHUNK + HALF
+LEFT = 2
 ROUND = 2
 
 
@@ -244,7 +247,7 @@
     return jnp.concatenate([high, low, high], axis=1)
 
 
-def whole_kernel(root, x_ref, own, factor_ref, got, relay, grams, la, xa, cross, lba, lb, xb, xba, acc, w,
+def whole_kernel(root, x_ref, own, factor_ref, got, w, relay, grams, la, xa, cross, lba, lb, xb, xba, acc,
                  half, quarter, rc, r1, r2, ry, half_b, quarter_b, rc_b, r1_b, r2_b, ry_b,
                  load_sem, go_sem, come_sem, hop_go_sem, hop_come_sem, send_sem, recv_sem):
     send = Sender(send_sem, recv_sem)
@@ -258,10 +261,18 @@
     chunk = lambda c: pl.ds(pl.multiple_of(c * CHUNK, CHUNK), CHUNK)
     pair = lambda c: pl.ds(pl.multiple_of(c * 2 * CHUNK, 2 * CHUNK), 2 * CHUNK)
 
-    def stream(c, ahead):
+    def stream(c, base):
         return pltpu.make_async_remote_copy(
-            src_ref=x_ref.at[chunk(c + ahead)], dst_ref=got.at[chunk(c)],
+            src_ref=x_ref.at[pl.ds(pl.multiple_of(c * CHUNK + base, HALF), CHUNK)], dst_ref=got.at[chunk(c)],
             send_sem=go_sem.at[c], recv_sem=come_sem.at[c], device_id=other, device_id_type=MESH)
+
+    def stream_half(start, base, sem):
+        return pltpu.make_async_remote_copy(
+            src_ref=x_ref.at[pl.ds(start + base, HALF)], dst_ref=got.at[pl.ds(start, HALF)],
+            send_sem=go_sem.at[sem], recv_sem=come_sem.at[sem], device_id=other, device_id_type=MESH)
+
+    a_halves = [stream_half(paired * CHUNK, 0, paired), stream_half(CROSS, 0, chunks)]
+    last_b = stream_half((paired - 1) * CHUNK, CROSS, paired - 1)
 
     def loop(begin, end, body):
         def step(c, carry):
@@ -285,11 +296,15 @@
 
     @pl.when(first)
     def _():
-        loop(0, direct, lambda c: stream(c, 0).start())
+        loop(0, paired, lambda c: stream(c, 0).start())
+        for copy in a_halves:
+            copy.start()
+        loop(paired + 1, direct, lambda c: stream(c, 0).start())
 
     @pl.when(second)
     def _():
-        loop(0, EARLY, lambda c: stream(c, paired).start())
+        loop(0, EARLY, lambda c: stream(c, CROSS).start())
+        last_b.start()
 
     acc[...] = jnp.zeros_like(acc)
 
@@ -307,7 +322,7 @@
 
     @pl.when(second)
     def _():
-        loop(EARLY, paired, lambda c: stream(c, paired).start())
+        loop(EARLY, paired - 1, lambda c: stream(c, CROSS).start())
 
     @pl.when(first)
     def _():
@@ -331,10 +346,9 @@
 
     acc[...] = jnp.zeros_like(acc)
 
-    def cross_one(c):
-        stream(c, 0).wait_recv()
-        there = got[chunk(c), :]
-        here = own[chunk(c + (1 - snap) * paired), :]
+    def add_cross(start, size, own_start):
+        there = got[pl.ds(start, size), :]
+        here = own[pl.ds(own_start, size), :]
         left = split(jnp.where(second, here, there))
         right = split(jnp.where(second, there, here))
         acc[...] += dot3(left, right, (0, 0))
@@ -344,7 +358,26 @@
         hop(0, 0).wait_recv()
         hop(1, 0).start()
 
-    loop(0, paired, cross_one)
+    def cross_one(c):
+        stream(c, 0).wait_recv()
+        start = pl.multiple_of(c * CHUNK, CHUNK)
+        add_cross(start, CHUNK, pl.multiple_of(start + (1 - snap) * CROSS, HALF))
+
+    loop(0, paired - 1, cross_one)
+    tail = (paired - 1) * CHUNK
+
+    @pl.when(first)
+    def _():
+        last_b.wait_recv()
+        add_cross(tail, HALF, tail + CROSS)
+
+    @pl.when(second)
+    def _():
+        stream(paired - 1, 0).wait_recv()
+        add_cross(tail, CHUNK, tail)
+        a_halves[0].wait_recv()
+        add_cross(paired * CHUNK, HALF, paired * CHUNK)
+
     scatter_sum(send, where, acc, half_b, quarter_b, rc_b, r1_b, r2_b, ry_b)
     put_piece(cross, 0, ry_b, (0, 2, 1, 3))
 
@@ -379,22 +412,32 @@
         factor_ref[n:, :] = lb[...].T / root
 
         def one(c):
+            @pl.when(c > paired // 2)
+            def _():
+                stream(2 * c, 0).wait_recv()
+
             @pl.when(c >= paired // 2)
             def _():
-                stream(2 * c, 0).wait_recv()
                 stream(2 * c + 1, 0).wait_recv()
 
             basis_one(c, thrice(own[pair(c), :]) + thrice(got[pair(c), :]), 6 * n)
 
-        loop(0, paired, one)
-        loop(0, paired, lambda c: stream(c, paired).wait_send())
+        a_halves[1].wait_recv()
+        loop(0, paired - LEFT, one)
+        for c in range(2 * (paired - LEFT), chunks):
+            stream(c, 0).wait_recv()
+        loop(0, paired - 1, lambda c: stream(c, CROSS).wait_send())
+        last_b.wait_send()
         for i in range(ROUND):
             hop(1, i).wait_send()
 
     @pl.when(first)
     def _():
-        loop(0, paired, lambda c: basis_one(c, thrice(own[pair(c), :]), 3 * n))
-        loop(0, direct, lambda c: stream(c, 0).wait_send())
+        loop(0, paired - LEFT, lambda c: basis_one(c, thrice(own[pair(c), :]), 3 * n))
+        loop(0, paired, lambda c: stream(c, 0).wait_send())
+        for copy in a_halves:
+            copy.wait_send()
+        loop(paired + 1, direct, lambda c: stream(c, 0).wait_send())
         for i in range(ROUND):
             hop(0, i).wait_send()
             hop(2, i).wait_send()
@@ -416,22 +459,69 @@
     dma = pltpu.SemaphoreType.DMA
     return pl.pallas_call(
         functools.partial(whole_kernel, root),
-        out_shape=(jax.ShapeDtypeStruct((count, n), f32), jax.ShapeDtypeStruct((2 * n, n), f32)),
+        out_shape=(jax.ShapeDtypeStruct((count, n), f32), jax.ShapeDtypeStruct((2 * n, n), f32),
+                   jax.ShapeDtypeStruct((count, n), f32), jax.ShapeDtypeStruct((n, 6 * n), jnp.bfloat16)),
         in_specs=[pl.BlockSpec(memory_space=pl.ANY)],
-        out_specs=(VMEM, VMEM),
-        scratch_shapes=[pltpu.VMEM((count, n), f32), pltpu.VMEM((ROUND, CHUNK, n), f32)]
+        out_specs=(VMEM,) * 4,
+        scratch_shapes=[pltpu.VMEM((ROUND, CHUNK, n), f32)]
         + [pltpu.VMEM((2, n, n), f32), square, square, pltpu.VMEM((1, n, n), f32)] + [square] * 5
-        + [pltpu.VMEM((n, 6 * n), jnp.bfloat16)] + sums + sums
-        + [dma((chunks,)), dma((chunks,)), dma((chunks,)), dma((2 * ROUND,)), dma((ROUND,)), dma((58,)), dma((58,))],
+        + sums + sums
+        + [dma((chunks,)), dma((chunks + 1,)), dma((chunks + 1,)), dma((2 * ROUND,)), dma((ROUND,)), dma((58,)), dma((58,))],
         compiler_params=pltpu.CompilerParams(
-            collective_id=0, has_side_effects=True, vmem_limit_bytes=40 << 20),
+            collective_id=0, has_side_effects=True, vmem_limit_bytes=30 << 20),
         cost_estimate=pl.CostEstimate(flops=130 << 30, bytes_accessed=400 << 20, transcendentals=0),
     )(snapshots)
 
 
+def finish_kernel(own, factor, got, w, basis_out, factor_out, stage, sems):
+    count, n = own.shape
+    size = 2 * CHUNK
+    done = count - LEFT * size
+    second = lax.axis_index("snap") == 1
+    copies = [
+        pltpu.make_async_copy(own.at[pl.ds(0, done)], basis_out.at[pl.ds(0, done)], sems.at[0]),
+        pltpu.make_async_copy(factor, factor_out, sems.at[1]),
+    ]
+    for copy in copies:
+        copy.start()
+    for i in range(LEFT):
+        at = pl.ds(done + i * size, size)
+
+        def make(values, width):
+            stage[i] = lax.dot_general(
+                jnp.concatenate(values, axis=1), w[:, :width], (((1,), (1,)), ((), ())),
+                preferred_element_type=jnp.float32)
+
+        @pl.when(second)
+        def _():
+            make(thrice(own[at, :]) + thrice(got[at, :]), 6 * n)
+
+        @pl.when(jnp.logical_not(second))
+        def _():
+            make(thrice(own[at, :]), 3 * n)
+
+        copies.append(pltpu.make_async_copy(stage.at[i], basis_out.at[at], sems.at[2 + i]))
+        copies[-1].start()
+    for copy in copies:
+        copy.wait()
+
+
+def finish(own, factor, got, w):
+    count, n = own.shape
+    here = pl.BlockSpec(memory_space=pl.ANY)
+    return pl.pallas_call(
+        finish_kernel,
+        out_shape=(jax.ShapeDtypeStruct(own.shape, own.dtype), jax.ShapeDtypeStruct(factor.shape, factor.dtype)),
+        in_specs=[VMEM] * 4,
+        out_specs=(here, here),
+        scratch_shapes=[pltpu.VMEM((LEFT, 2 * CHUNK, n), jnp.float32), pltpu.SemaphoreType.DMA((2 + LEFT,))],
+        compiler_params=pltpu.CompilerParams(vmem_limit_bytes=30 << 20),
+    )(own, factor, got, w)
+
+
 def on_device(snapshots):
     root_rows = float(snapshots.shape[0] * lax.axis_size("dof")) ** 0.5
-    return tuple(whole(snapshots, root_rows))
+    return tuple(finish(*whole(snapshots, root_rows)))
 
 
 def solution(mesh):

time: 188 us -> 181 us (0.963)
  local copies, waits for them, and re-layouts: 4.72 us -> 0 us
  Pallas kernels: 182 us -> 180 us
    pallas_call x1, Pallas kernels: 182 us -> 175 us  [whole(): pl.pallas_call(functools.partial(whole_kernel, root), out_shape=(jax.Shap...]
    unnamed x2 -> x0, local copies, waits for them, and re-layouts: 4.72 us -> none
    pallas_call x0 -> x1, Pallas kernels: none -> 4.66 us  [finish(): pl.pallas_call(finish_kernel, out_shape=(jax.ShapeDtypeStruct(own.shape,...]
where the time goes in v4:
time: 181 us
  Pallas kernels  180 us (99%)
    pallas_call x1, Pallas kernels, whole(): pl.pallas_call(functools.partial(whole_kernel, root), out_shape=(jax.Shap...  175 us
    pallas_call x1, Pallas kernels, finish(): pl.pallas_call(finish_kernel, out_shape=(jax.ShapeDtypeStruct(own.shape,...  4.66 us

profile of v4, /device:TPU:9, one launch (start us, length us, event | category | flops | bytes accessed | tf_op | source)
XLA Modules:
  0.0 180.6 jit_solution(4025701118856987549)
XLA Ops:
  0.6 175.1 %shard_map.30 = (f32[4096,512]{1,0:T(8,128)S(1)}, f32[1024,512]{1,0:T(8,128)S(1)}, f32[4096,512]{1,0:T(8,128)S(1)}, bf16[512,3072]{1,0:T(8,128)(2,1)S(1)}) custom-call(f32[4096,512]{1,0:T(8,128)} %x_ref.1), custom_call_target="tpu_custom_call" | custom-call | flops 139586437120 | bytes 419430400 | tf_op jit(solution)/shard_map/pallas_call | solution.py:460
  175.7 4.7 %shard_map.31 = (f32[4096,512]{1,0:T(8,128)}, f32[1024,512]{1,0:T(8,128)}) custom-call(f32[4096,512]{1,0:T(8,128)S(1)} %get-tuple-element.6.own, f32[1024,512]{1,0:T(8,128)S(1)} %get-tuple-element.7.factor, f32[4096,512]{1,0:T(8,128)S(1)} %get-tuple-element.8.got, bf16[512,3072]{1,0:T(8,128)(2,1)S(1)} %get-tuple-element.9.w), custom_call_target="tpu_custom_call" | custom-call | tf_op jit(solution)/shard_map/pallas_call | solution.py:512

commit v5 on v4

--- a/solution.py
+++ b/solution.py
@@ -8,14 +8,15 @@
 from jax.sharding import PartitionSpec as P
 
 MESH = pl.DeviceIdType.MESH
-HI = lax.Precision.HIGHEST
 T = 128
 
 def dot_nt(a, b):
-    return lax.dot_general(a, b, (((1,), (1,)), ((), ())), preferred_element_type=jnp.float32, precision=HI)
+    return dot4(split(a), split(b), (1, 1))
+
 
 def dot_nn(a, b):
-    return lax.dot_general(a, b, (((1,), (0,)), ((), ())), preferred_element_type=jnp.float32, precision=HI)
+    return dot4(split(a), split(b), (1, 0))
+
 
 def eliminate(block):
     sub = lax.broadcasted_iota(jnp.int32, (8, T), 0)
@@ -204,14 +205,23 @@
     for k in (2, 1, 3):
         jobs += [(lpart, lpart, over_z[k - 1]), (rpart, rpart, over_x[k - 1])]
     send.run(jobs)
-    lpart = out_ref.at[:, rows(core * h + x * q, q), left]
-    rpart = out_ref.at[:, rows(core * h + z * q, q), right]
-    jobs = []
-    for k in (2, 1, 3):
-        jobs += [(lpart, lpart, over_x[k - 1]), (rpart, rpart, over_z[k - 1])]
-    send.run(jobs)
-    part = out_ref.at[:, rows(core * h, h)]
-    send.run([(part, part, over_core[0])])
+    block = (
+        lambda k: out_ref.at[:, rows(core * h + lax.rem(x + k, 4) * q, q), left],
+        lambda k: out_ref.at[:, rows(core * h + lax.rem(z + k, 4) * q, q), right],
+    )
+    landing = []
+    for k in (1, 3, 2):
+        for side, over in ((0, over_x), (1, over_z)):
+            landing.append((send.start(block[side](0), block[side](0), over[k - 1]), side, k))
+    passing = [send.start(block[side](0), block[side](0), over_core[0]) for side in (0, 1)]
+    for copy, side, k in landing:
+        copy.wait_recv()
+        part = block[side](4 - k)
+        passing.append(send.start(part, part, over_core[0]))
+    for copy, _, _ in landing:
+        copy.wait_send()
+    for copy in passing:
+        copy.wait()
 
 
 def split(x):
@@ -219,10 +229,10 @@
     return high, (x - high.astype(jnp.float32)).astype(jnp.bfloat16)
 
 
-def dot3(a, b, over):
+def dot4(a, b, over):
     dims = ((over[:1], over[1:]), ((), ()))
     dot = lambda l, r: lax.dot_general(l, r, dims, preferred_element_type=jnp.float32)
-    return dot(a[0], b[0]) + (dot(a[0], b[1]) + dot(a[1], b[0]))
+    return dot(a[0], b[0]) + (dot(a[0], b[1]) + (dot(a[1], b[0]) + dot(a[1], b[1])))
 
 
 CHUNK = 256
@@ -311,7 +321,8 @@
     def gram_one(c):
         load(c).wait()
         high, low = split(own[chunk(c), :])
-        acc[...] += dot_tn(high, high * jnp.bfloat16(0.5)) + dot_tn(high, low)
+        half_high, half_low = high * jnp.bfloat16(0.5), low * jnp.bfloat16(0.5)
+        acc[...] += dot_tn(high, half_high) + dot_tn(high, low) + dot_tn(low, half_low)
 
     loop(0, chunks, gram_one)
     acc[...] = acc[...] + acc[...].T
@@ -351,7 +362,7 @@
         here = own[pl.ds(own_start, size), :]
         left = split(jnp.where(second, here, there))
         right = split(jnp.where(second, there, here))
-        acc[...] += dot3(left, right, (0, 0))
+        acc[...] += dot4(left, right, (0, 0))
 
     @pl.when(second)
     def _():
@@ -466,7 +477,7 @@
         scratch_shapes=[pltpu.VMEM((ROUND, CHUNK, n), f32)]
         + [pltpu.VMEM((2, n, n), f32), square, square, pltpu.VMEM((1, n, n), f32)] + [square] * 5
         + sums + sums
-        + [dma((chunks,)), dma((chunks + 1,)), dma((chunks + 1,)), dma((2 * ROUND,)), dma((ROUND,)), dma((58,)), dma((58,))],
+        + [dma((chunks,)), dma((chunks + 1,)), dma((chunks + 1,)), dma((2 * ROUND,)), dma((ROUND,)), dma((72,)), dma((72,))],
         compiler_params=pltpu.CompilerParams(
             collective_id=0, has_side_effects=True, vmem_limit_bytes=30 << 20),
         cost_estimate=pl.CostEstimate(flops=130 << 30, bytes_accessed=400 << 20, transcendentals=0),

time: 181 us -> 177 us (0.978)
  Pallas kernels: 180 us -> 176 us
    pallas_call x1, Pallas kernels: 175 us -> 171 us  [whole(): pl.pallas_call(functools.partial(whole_kernel, root), out_shape=(jax.Shap...]
where the time goes in v5:
time: 177 us
  Pallas kernels  176 us (99%)
    pallas_call x1, Pallas kernels, whole(): pl.pallas_call(functools.partial(whole_kernel, root), out_shape=(jax.Shap...  171 us
    pallas_call x1, Pallas kernels, finish(): pl.pallas_call(finish_kernel, out_shape=(jax.ShapeDtypeStruct(own.shape,...  4.87 us

profile of v5, /device:TPU:9, one launch (start us, length us, event | category | flops | bytes accessed | tf_op | source)
XLA Modules:
  0.0 176.8 jit_solution(16415408530020679610)
XLA Ops:
  0.6 171.1 %shard_map.30 = (f32[4096,512]{1,0:T(8,128)S(1)}, f32[1024,512]{1,0:T(8,128)S(1)}, f32[4096,512]{1,0:T(8,128)S(1)}, bf16[512,3072]{1,0:T(8,128)(2,1)S(1)}) custom-call(f32[4096,512]{1,0:T(8,128)} %x_ref.1), custom_call_target="tpu_custom_call" | custom-call | flops 139586437120 | bytes 419430400 | tf_op jit(solution)/shard_map/pallas_call | solution.py:471
  171.7 4.9 %shard_map.31 = (f32[4096,512]{1,0:T(8,128)}, f32[1024,512]{1,0:T(8,128)}) custom-call(f32[4096,512]{1,0:T(8,128)S(1)} %get-tuple-element.6.own, f32[1024,512]{1,0:T(8,128)S(1)} %get-tuple-element.7.factor, f32[4096,512]{1,0:T(8,128)S(1)} %get-tuple-element.8.got, bf16[512,3072]{1,0:T(8,128)(2,1)S(1)} %get-tuple-element.9.w), custom_call_target="tpu_custom_call" | custom-call | tf_op jit(solution)/shard_map/pallas_call | solution.py:523

commit v6 on v5

--- a/solution.py
+++ b/solution.py
@@ -154,7 +154,7 @@
     return pl.ds(pl.multiple_of(start, size), size)
 
 
-def scatter_sum(send, where, p_ref, half, quarter, rc, r1, r2, ry):
+def scatter_sum(send, where, p_ref, half, quarter, rc, r1, r2, ry, behind):
     over_core, over_x, over_z, down = where
     z, x, y, core = place()
     n = p_ref.shape[0]
@@ -178,7 +178,10 @@
     ry[y, 1] = (quarter[1, rows(x * s, s), :] + r2[1, 1]) + (r2[1, 0] + r2[1, 2])
     for k in (0, 1, 2):
         slot = ry.at[lax.rem(y + k, 4)]
-        send.run([(slot, slot, down)])
+        copy = send.start(slot, slot, down)
+        if k == 2:
+            behind()
+        copy.wait()
 
 
 def put_piece(out_ref, block, ry, slots):
@@ -237,8 +240,8 @@
 
 CHUNK = 256
 EARLY = 2
-HALF = CHUNK // 2
-CROSS = 8 * CHUNK + HALF
+PART = CHUNK // 4
+CROSS = 8 * CHUNK + PART
 LEFT = 2
 ROUND = 2
 
@@ -273,16 +276,16 @@
 
     def stream(c, base):
         return pltpu.make_async_remote_copy(
-            src_ref=x_ref.at[pl.ds(pl.multiple_of(c * CHUNK + base, HALF), CHUNK)], dst_ref=got.at[chunk(c)],
+            src_ref=x_ref.at[pl.ds(pl.multiple_of(c * CHUNK + base, PART), CHUNK)], dst_ref=got.at[chunk(c)],
             send_sem=go_sem.at[c], recv_sem=come_sem.at[c], device_id=other, device_id_type=MESH)
 
-    def stream_half(start, base, sem):
+    def stream_part(start, base, size, sem):
         return pltpu.make_async_remote_copy(
-            src_ref=x_ref.at[pl.ds(start + base, HALF)], dst_ref=got.at[pl.ds(start, HALF)],
+            src_ref=x_ref.at[pl.ds(start + base, size)], dst_ref=got.at[pl.ds(start, size)],
             send_sem=go_sem.at[sem], recv_sem=come_sem.at[sem], device_id=other, device_id_type=MESH)
 
-    a_halves = [stream_half(paired * CHUNK, 0, paired), stream_half(CROSS, 0, chunks)]
-    last_b = stream_half((paired - 1) * CHUNK, CROSS, paired - 1)
+    a_parts = [stream_part(paired * CHUNK, 0, PART, paired), stream_part(CROSS, 0, CHUNK - PART, chunks)]
+    last_b = stream_part((paired - 1) * CHUNK, CROSS, CHUNK - PART, paired - 1)
 
     def loop(begin, end, body):
         def step(c, carry):
@@ -307,7 +310,7 @@
     @pl.when(first)
     def _():
         loop(0, paired, lambda c: stream(c, 0).start())
-        for copy in a_halves:
+        for copy in a_parts:
             copy.start()
         loop(paired + 1, direct, lambda c: stream(c, 0).start())
 
@@ -327,19 +330,19 @@
     loop(0, chunks, gram_one)
     acc[...] = acc[...] + acc[...].T
 
-    scatter_sum(send, where, acc, half, quarter, rc, r1, r2, ry)
+    def behind_first():
+        @pl.when(second)
+        def _():
+            loop(EARLY, paired - 1, lambda c: stream(c, CROSS).start())
+
+        @pl.when(first)
+        def _():
+            for i in range(ROUND):
+                hop(0, i).start()
+
+    scatter_sum(send, where, acc, half, quarter, rc, r1, r2, ry, behind_first)
     put_piece(grams, 0, ry, (0, 2))
     put_piece(grams, 1, ry, (1, 3))
-
-    @pl.when(second)
-    def _():
-        loop(EARLY, paired - 1, lambda c: stream(c, CROSS).start())
-
-    @pl.when(first)
-    def _():
-        for i in range(ROUND):
-            hop(0, i).start()
-
     gather_rows(send, where, grams)
     acc[...] = grams[0]
     factor_into(acc, la, xa, n)
@@ -372,7 +375,7 @@
     def cross_one(c):
         stream(c, 0).wait_recv()
         start = pl.multiple_of(c * CHUNK, CHUNK)
-        add_cross(start, CHUNK, pl.multiple_of(start + (1 - snap) * CROSS, HALF))
+        add_cross(start, CHUNK, pl.multiple_of(start + (1 - snap) * CROSS, PART))
 
     loop(0, paired - 1, cross_one)
     tail = (paired - 1) * CHUNK
@@ -380,29 +383,29 @@
     @pl.when(first)
     def _():
         last_b.wait_recv()
-        add_cross(tail, HALF, tail + CROSS)
+        add_cross(tail, CHUNK - PART, tail + CROSS)
 
     @pl.when(second)
     def _():
         stream(paired - 1, 0).wait_recv()
         add_cross(tail, CHUNK, tail)
-        a_halves[0].wait_recv()
-        add_cross(paired * CHUNK, HALF, paired * CHUNK)
-
-    scatter_sum(send, where, acc, half_b, quarter_b, rc_b, r1_b, r2_b, ry_b)
+        a_parts[0].wait_recv()
+        add_cross(paired * CHUNK, PART, paired * CHUNK)
+
+    def behind_second():
+        @pl.when(second)
+        def _():
+            for i in range(1, ROUND):
+                hop(0, i).wait_recv()
+                hop(1, i).start()
+
+        @pl.when(first)
+        def _():
+            hop(1, 0).wait_recv()
+            hop(2, 0).start()
+
+    scatter_sum(send, where, acc, half_b, quarter_b, rc_b, r1_b, r2_b, ry_b, behind_second)
     put_piece(cross, 0, ry_b, (0, 2, 1, 3))
-
-    @pl.when(second)
-    def _():
-        for i in range(1, ROUND):
-            hop(0, i).wait_recv()
-            hop(1, i).start()
-
-    @pl.when(first)
-    def _():
-        hop(1, 0).wait_recv()
-        hop(2, 0).start()
-
     gather_rows(send, where, cross)
 
     @pl.when(first)
@@ -433,7 +436,7 @@
 
             basis_one(c, thrice(own[pair(c), :]) + thrice(got[pair(c), :]), 6 * n)
 
-        a_halves[1].wait_recv()
+        a_parts[1].wait_recv()
         loop(0, paired - LEFT, one)
         for c in range(2 * (paired - LEFT), chunks):
             stream(c, 0).wait_recv()
@@ -446,7 +449,7 @@
     def _():
         loop(0, paired - LEFT, lambda c: basis_one(c, thrice(own[pair(c), :]), 3 * n))
         loop(0, paired, lambda c: stream(c, 0).wait_send())
-        for copy in a_halves:
+        for copy in a_parts:
             copy.wait_send()
         loop(paired + 1, direct, lambda c: stream(c, 0).wait_send())
         for i in range(ROUND):

time: 177 us -> 178 us (level)
  no operation moved by 1% of the time
where the time goes in v6:
time: 178 us
  Pallas kernels  177 us (99%)
    pallas_call x1, Pallas kernels, whole(): pl.pallas_call(functools.partial(whole_kernel, root), out_shape=(jax.Shap...  172 us
    pallas_call x1, Pallas kernels, finish(): pl.pallas_call(finish_kernel, out_shape=(jax.ShapeDtypeStruct(own.shape,...  4.87 us

profile of v6, /device:TPU:9, one launch (start us, length us, event | category | flops | bytes accessed | tf_op | source)
XLA Modules:
  0.0 178.1 jit_solution(14379390981831278253)
XLA Ops:
  0.6 172.5 %shard_map.30 = (f32[4096,512]{1,0:T(8,128)S(1)}, f32[1024,512]{1,0:T(8,128)S(1)}, f32[4096,512]{1,0:T(8,128)S(1)}, bf16[512,3072]{1,0:T(8,128)(2,1)S(1)}) custom-call(f32[4096,512]{1,0:T(8,128)} %x_ref.1), custom_call_target="tpu_custom_call" | custom-call | flops 139586437120 | bytes 419430400 | tf_op jit(solution)/shard_map/pallas_call | solution.py:474
  173.1 4.9 %shard_map.31 = (f32[4096,512]{1,0:T(8,128)}, f32[1024,512]{1,0:T(8,128)}) custom-call(f32[4096,512]{1,0:T(8,128)S(1)} %get-tuple-element.6.own, f32[1024,512]{1,0:T(8,128)S(1)} %get-tuple-element.7.factor, f32[4096,512]{1,0:T(8,128)S(1)} %get-tuple-element.8.got, bf16[512,3072]{1,0:T(8,128)(2,1)S(1)} %get-tuple-element.9.w), custom_call_target="tpu_custom_call" | custom-call | tf_op jit(solution)/shard_map/pallas_call | solution.py:526

commit v7 on v6

--- a/solution.py
+++ b/solution.py
@@ -392,20 +392,19 @@
         a_parts[0].wait_recv()
         add_cross(paired * CHUNK, PART, paired * CHUNK)
 
-    def behind_second():
-        @pl.when(second)
-        def _():
-            for i in range(1, ROUND):
-                hop(0, i).wait_recv()
-                hop(1, i).start()
-
-        @pl.when(first)
-        def _():
-            hop(1, 0).wait_recv()
-            hop(2, 0).start()
-
-    scatter_sum(send, where, acc, half_b, quarter_b, rc_b, r1_b, r2_b, ry_b, behind_second)
+    scatter_sum(send, where, acc, half_b, quarter_b, rc_b, r1_b, r2_b, ry_b, lambda: None)
     put_piece(cross, 0, ry_b, (0, 2, 1, 3))
+    @pl.when(second)
+    def _():
+        for i in range(1, ROUND):
+            hop(0, i).wait_recv()
+            hop(1, i).start()
+
+    @pl.when(first)
+    def _():
+        hop(1, 0).wait_recv()
+        hop(2, 0).start()
+
     gather_rows(send, where, cross)
 
     @pl.when(first)

time: 178 us -> 178 us (level)
  no operation moved by 1% of the time
where the time goes in v7:
time: 178 us
  Pallas kernels  177 us (99%)
    pallas_call x1, Pallas kernels, whole(): pl.pallas_call(functools.partial(whole_kernel, root), out_shape=(jax.Shap...  172 us
    pallas_call x1, Pallas kernels, finish(): pl.pallas_call(finish_kernel, out_shape=(jax.ShapeDtypeStruct(own.shape,...  4.87 us

profile of v7, /device:TPU:9, one launch (start us, length us, event | category | flops | bytes accessed | tf_op | source)
XLA Modules:
  0.0 178.0 jit_solution(13757051731088188307)
XLA Ops:
  0.6 172.3 %shard_map.30 = (f32[4096,512]{1,0:T(8,128)S(1)}, f32[1024,512]{1,0:T(8,128)S(1)}, f32[4096,512]{1,0:T(8,128)S(1)}, bf16[512,3072]{1,0:T(8,128)(2,1)S(1)}) custom-call(f32[4096,512]{1,0:T(8,128)} %x_ref.1), custom_call_target="tpu_custom_call" | custom-call | flops 139586437120 | bytes 419430400 | tf_op jit(solution)/shard_map/pallas_call | solution.py:473
  173.0 4.9 %shard_map.31 = (f32[4096,512]{1,0:T(8,128)}, f32[1024,512]{1,0:T(8,128)}) custom-call(f32[4096,512]{1,0:T(8,128)S(1)} %get-tuple-element.6.own, f32[1024,512]{1,0:T(8,128)S(1)} %get-tuple-element.7.factor, f32[4096,512]{1,0:T(8,128)S(1)} %get-tuple-element.8.got, bf16[512,3072]{1,0:T(8,128)(2,1)S(1)} %get-tuple-element.9.w), custom_call_target="tpu_custom_call" | custom-call | tf_op jit(solution)/shard_map/pallas_call | solution.py:525
